TPU v7x, 256 devices: a whole 4x4x8 slice. The times are simulated.
256 devices in a mesh: sky: 64 (over x, z, core), band: 4 (over y).
Axes of the slice: x: 4, y: 4, z: 8, core: 2. Of those that a mesh axis runs over, the one named last changes fastest.
Arguments:
- raw_blocks: bfloat16 [168, 1376256], P(None, ('sky', 'band')), may hold values from -6 to 6
- patch_of_block: int32 [8192, 1], P(('sky', 'band')), may hold values from 0 to 63; in each aligned block of 32 rows (0 to 31, 32 to 63, ...) at most 2 rows name the same one
- cell_of_block: int32 [8192], P(('sky', 'band')), may hold values from 0 to 15
- band_of_block: int32 [8192], P(('sky', 'band')), may hold values from 0 to 5
- block_weight: bfloat16 [8192], P(('sky', 'band')), may hold values from 0.25 to 4
- basis_coef: bfloat16 [8192, 3], P(('sky', 'band')), may hold values from 0.25 to 1
- row_basis: float32 [3, 41], replicated, may hold values from -1 to 1
- col_basis: float32 [3, 41], replicated, may hold values from -1 to 1
- band_gain: float32 [6], replicated, may hold values from 0.5 to 2
- filter_taps: float32 [41], replicated, may hold values from -1 to 1
Outputs:
- detection: float32 [64, 512, 512], P('sky', 'band')
Inputs may be any that keep to these rules, and one draw needn't show every extreme that they name: `patch_of_block`: of the 32 blocks of one device at most 2 intersect one patch, and on some device exactly 2 do.
All inputs are finite; a program needn't handle non-finite values.
Results may differ from a plain program's by a relative error of at most 0.015.
Values may be sent and summed in bfloat16 or wider, within the bound.
A program may use at most 128 MiB of HBM per device.

v0:
```python
import jax
import jax.numpy as jnp
from jax import lax
from jax.sharding import PartitionSpec as P

BANDS = 6
CR = 4
CC = 4
CELLS = 16


def extended(block, sides, width):
    for axis, dim in sides:
        count = lax.axis_size(axis)
        forward = [(i, i + 1) for i in range(count - 1)]
        backward = [(target, source) for source, target in forward]
        low = lax.ppermute(
            lax.slice_in_dim(block, block.shape[dim] - width, None, axis=dim), axis, forward
        )
        high = lax.ppermute(lax.slice_in_dim(block, 0, width, axis=dim), axis, backward)
        block = jnp.concatenate([low, block, high], axis=dim)
    return block


def toeplitz(tap_values, rows_out):
    tap_count = tap_values.shape[0]
    period = jnp.concatenate([tap_values, jnp.zeros((rows_out,), tap_values.dtype)])
    flat_row = jnp.tile(period, rows_out)[: rows_out * (rows_out + tap_count - 1)]
    return flat_row.reshape(rows_out, rows_out + tap_count - 1)


def kernel_stack(basis_taps, rows_out):
    return jnp.stack(
        [toeplitz(basis_taps[k], rows_out) for k in range(basis_taps.shape[0])]
    ).astype(jnp.bfloat16)


def match_one(row_kernels, col_kernels, raw_block, coefficient):
    sectioned = jnp.einsum(
        "kip,pq->kiq", row_kernels, raw_block, preferred_element_type=jnp.float32
    ).astype(jnp.bfloat16)
    basis_terms = jnp.einsum(
        "kiq,kjq->kij", sectioned, col_kernels, preferred_element_type=jnp.float32
    )
    return jnp.sum(coefficient.astype(jnp.float32)[:, None, None] * basis_terms, axis=0).astype(
        jnp.bfloat16
    )


def match_many(row_kernels, col_kernels, raw_many, coef_many):

    def single(block_pair):
        return match_one(row_kernels, col_kernels, block_pair[0], block_pair[1])

    return lax.map(single, (raw_many, coef_many), batch_size=16)


def local(
    raw_blocks,
    patch_of_block,
    cell_of_block,
    band_of_block,
    block_weight,
    basis_coef,
    row_basis,
    col_basis,
    band_gain,
    filter_taps,
):
    sky_count = lax.axis_size("sky")
    band_count = lax.axis_size("band")
    margin_side = raw_blocks.shape[0]
    block_count = raw_blocks.shape[1] // margin_side
    basis_count = row_basis.shape[0]
    radius = (filter_taps.shape[0] - 1) // 2
    block_side = margin_side - 2 * radius
    capacity = max(2, (2 * block_count + sky_count - 1) // sky_count)
    slot_count = sky_count * capacity
    row_kernels = kernel_stack(row_basis, block_side)
    col_kernels = kernel_stack(col_basis, block_side)
    block_major = raw_blocks.reshape(margin_side, block_count, margin_side).transpose(1, 0, 2)
    owner_patch = patch_of_block[:, 0]
    positions = jnp.arange(block_count, dtype=jnp.int32)
    earlier_peer = (owner_patch[:, None] == owner_patch[None, :]) & (
        positions[None, :] < positions[:, None]
    )
    rank_within = jnp.sum(earlier_peer.astype(jnp.int32), axis=1)
    slot_index = owner_patch * capacity + rank_within
    wanted = slot_index[None, :] == jnp.arange(slot_count, dtype=jnp.int32)[:, None]
    source = jnp.sum(jnp.where(wanted, positions[None, :], 0), axis=1) + jnp.where(
        jnp.any(wanted, axis=1), 0, block_count
    )
    details = jnp.concatenate(
        [
            block_weight[:, None],
            basis_coef,
            cell_of_block[:, None].astype(jnp.bfloat16),
            band_of_block[:, None].astype(jnp.bfloat16),
        ],
        axis=1,
    )
    detail_width = details.shape[1]
    outgoing_details = jnp.take(details, source, axis=0, mode="fill", fill_value=0).reshape(
        sky_count, capacity, detail_width
    )
    outgoing = jnp.take(block_major, source, axis=0, mode="fill", fill_value=0).reshape(
        sky_count, capacity, margin_side, margin_side
    )
    raw_piece = lax.all_to_all(outgoing, "sky", split_axis=0, concat_axis=0, tiled=True)
    detail_piece = lax.all_to_all(outgoing_details, "sky", split_axis=0, concat_axis=0, tiled=True)
    leading = raw_piece.shape[:2]
    flat_raw = raw_piece.reshape((-1, margin_side, margin_side))
    flat_coef = detail_piece.reshape((-1, detail_width))[:, 1 : 1 + basis_count]
    matched_piece = match_many(row_kernels, col_kernels, flat_raw, flat_coef)
    arrived = matched_piece.reshape(leading + (block_side, block_side))
    flat_match = arrived.reshape(slot_count, block_side * block_side)
    flat_info = detail_piece.reshape(slot_count, detail_width)
    cell_id = flat_info[:, basis_count + 1].astype(jnp.int32)
    band_id = flat_info[:, basis_count + 2].astype(jnp.int32)
    target_bin = band_id * CELLS + cell_id
    bin_ids = jnp.arange(BANDS * CELLS, dtype=jnp.int32)
    spread = jnp.where(
        target_bin[None, :] == bin_ids[:, None], flat_info[None, :, 0], jnp.zeros((), jnp.bfloat16)
    )
    totals = jnp.dot(spread, flat_match, preferred_element_type=jnp.float32).reshape(
        BANDS, CR, CC, block_side, block_side
    )
    weights = jnp.sum(spread.astype(jnp.float32), axis=1).reshape(BANDS, CR, CC)
    rows_here = CR // band_count
    full_totals, full_weights = lax.psum((totals, weights), "band")
    row_start = lax.axis_index("band") * rows_here
    part_totals = lax.dynamic_slice_in_dim(full_totals, row_start, rows_here, 1)
    part_weights = lax.dynamic_slice_in_dim(full_weights, row_start, rows_here, 1)
    coadd_image = part_totals / jnp.maximum(part_weights, 1.0)[..., None, None]
    combined = jnp.sum(band_gain[:, None, None, None, None] * coadd_image, axis=0)
    patch_image = (
        combined.transpose(0, 2, 1, 3)
        .reshape(rows_here * block_side, CC * block_side)
        .astype(jnp.bfloat16)
    )
    padded = extended(patch_image, (("band", 0),), radius)
    filter_bf16 = filter_taps.astype(jnp.bfloat16)
    row_filter = toeplitz(filter_bf16, rows_here * block_side)
    smoothed = jnp.dot(row_filter, padded, preferred_element_type=jnp.float32).astype(jnp.bfloat16)
    col_filter = toeplitz(filter_bf16, CC * block_side)[:, radius : radius + CC * block_side].T
    detection = jnp.dot(smoothed, col_filter, preferred_element_type=jnp.float32)
    return detection[None]


def solution(mesh):
    return jax.shard_map(
        local,
        mesh=mesh,
        in_specs=(
            P(None, ("sky", "band")),
            P(("sky", "band"), None),
            P(("sky", "band")),
            P(("sky", "band")),
            P(("sky", "band")),
            P(("sky", "band"), None),
            P(),
            P(),
            P(),
            P(),
        ),
        out_specs=P("sky", "band", None),
        check_vma=False,
    )
```

profile of v0, /device:TPU:16, one launch (start us, length us, event | category | flops | bytes accessed | tf_op | source)
XLA Modules:
  0.0 556.3 jit_solution(15665514603310065326)
XLA Ops:
  6.5 0.9 convert_reduce_fusion.1
  11.4 11.9 %all-to-all-start = ((bf16[64,2,6]{2,1,0:T(2,128)(2,1)}), bf16[64,2,6]{2,1,0:T(2,128)(2,1)S(1)}, u32[]{:S(2)}, u32[]{:S(2)}) async-start(bf16[64,2,6]{2,1,0:T(2,128)(2,1)} %broadcast_select_fusion.1), calls=%async_computation | async-start | bytes 65536 | tf_op jit(solution)/shard_map/all_to_all | solution.py:110
  23.4 9.8 %reshape.164 = bf16[168,32,168]{2,1,0:T(8,128)(2,1)} reshape(bf16[168,5376]{1,0:T(8,128)(2,1)} %param.12) | data formatting | bytes 3612672 | tf_op jit(solution)/shard_map/reshape | solution.py:81
  33.1 3.3 copy.104
  36.4 7.5 %gather_fusion.1 = bf16[128,168,168]{2,1,0:T(8,128)(2,1)} fusion(bf16[32,168,168]{2,1,0:T(8,128)(2,1)S(1)} %bitcast.114, s32[1024]{0:T(1024)S(1)} %pad_clamp_fusion), kind=kCustom, calls=%fused_computation.1 | custom fusion | bytes 14451200 | tf_op jit(solution)/shard_map/jit(_take)/gather | solution.py:106
  44.0 10.2 %broadcast_select_fusion = bf16[64,2,168,168]{3,2,1,0:T(8,128)(2,1)} fusion(bf16[64,2,168,168]{3,2,1,0:T(8,128)(2,1)} %bitcast.115, pred[64,2]{1,0:T(8,128)(4,1)S(1)} %compare_and_fusion), kind=kLoop, calls=%fused_computation.15 | loop fusion | flops 3612672 | bytes 14450816 | tf_op jit(solution)/shard_map/jit(_take)/select_n | solution.py:106
  54.2 10.7 %all-to-all-start.1 = ((bf16[64,2,168,168]{3,2,1,0:T(8,128)(2,1)}), bf16[64,2,168,168]{3,2,1,0:T(8,128)(2,1)}, u32[]{:S(2)}, u32[]{:S(2)}) async-start(bf16[64,2,168,168]{3,2,1,0:T(8,128)(2,1)} %broadcast_select_fusion), calls=%async_computation.1 | async-start | bytes 22020096 | tf_op jit(solution)/shard_map/all_to_all | solution.py:109
  69.4 236.5 %all-to-all-done.1 = bf16[64,2,168,168]{3,2,1,0:T(8,128)(2,1)} async-done(((bf16[64,2,168,168]{3,2,1,0:T(8,128)(2,1)}), bf16[64,2,168,168]{3,2,1,0:T(8,128)(2,1)}, u32[]{:S(2)}, u32[]{:S(2)}) %all-to-all-start.1) | async-done | bytes 7225376 | tf_op jit(solution)/shard_map/all_to_all | solution.py:109
  305.9 15.3 %copy.79 = bf16[64,2,168,168]{2,3,1,0:T(8,128)(2,1)} copy(bf16[64,2,168,168]{3,2,1,0:T(8,128)(2,1)} %all-to-all-done.1) | data formatting | bytes 14450688 | tf_op jit(solution)/shard_map/all_to_all | solution.py:109
  321.3 32.1 %while.10 = (s32[]{:T(128)}, bf16[8,16,128,128]{3,2,1,0:T(8,128)(2,1)}, bf16[8,16,3]{1,2,0:T(4,128)(2,1)S(1)}, bf16[8,16,168,168]{2,3,1,0:T(8,128)(2,1)}, bf16[3...) while((s32[]{:T(128)}, bf16[8,16,128,128]{3,2,1,0:T(8,128)(2,1)}, ...), condition=%wide.region_5.6_spmd, body=%wide.region_3.5_spmd.sunk | while | flops 613400640 | bytes 3208753 | solution.py:55
  321.3 3.1 fusion.56
  325.3 3.1 fusion.56
  329.3 3.1 fusion.56
  333.3 3.1 fusion.56
  336.4 0.9 bitcast_dynamic-update-slice_fusion.2
  337.3 3.1 fusion.56
  341.3 3.1 fusion.56
  345.3 3.1 fusion.56
  348.4 0.9 bitcast_dynamic-update-slice_fusion.2
  349.3 3.1 fusion.56
  352.5 0.9 bitcast_dynamic-update-slice_fusion.2
  353.4 7.7 %copy.103 = bf16[16,8,128,128]{3,1,2,0:T(8,128)(2,1)} copy(bf16[16,8,128,128]{3,2,1,0:T(8,128)(2,1)} %bitcast.119) | data formatting | bytes 8388608
  361.1 6.3 %copy.83 = bf16[16384,128]{1,0:T(8,128)(2,1)} copy(bf16[16384,128]{0,1:T(8,128)(2,1)} %bitcast.117) | data formatting | bytes 8388608 | tf_op jit(solution)/shard_map/dot_general | solution.py:125
  367.4 7.0 %fusion.32 = f32[6,4,4,128,128]{4,0,3,2,1:T(8,128)} fusion(bf16[128,128,128,1,1]{2,1,0,4,3:T(8,128)(2,1)} %bitcast.116, s32[6,4,4]{0,2,1:T(4,128)S(1)} %multiply_add_fusion, s32[128]{0:T(128)S(1)} %add_reduce_fusion, bf16[128]{0:T(256)(128)(2,1)S(1)} %slice_reduce_fusion), kind=kOutput, calls=%fused_computation.38 | convolution fusion | flops 402677760 | bytes 10486912 | tf_op jit(solution)/shard_map/dot_general | solution.py:125
  374.7 8.5 %psum.15 = f32[6,4,4]{0,2,1:T(4,128)S(1)} all-reduce(f32[6,4,4]{0,2,1:T(4,128)S(1)} %copy.84), channel_id=1, replica_groups=mesh['sky'=64,'band'=4] {'band'}, use_global_device_ids=true, to_apply=%region_8.9 | all-reduce | flops 96 | bytes 768 | tf_op jit(solution)/shard_map/psum | solution.py:130
  383.3 152.8 %all-reduce.10.cloned.1.call-done = f32[6,4,4,128,128]{4,0,3,2,1:T(8,128)} async-done(((f32[6,4,4,128,128]{4,0,3,2,1:T(8,128)}), f32[6,4,4,128,128]{4,0,3,2,1:T(8,128)}) %all-reduce.10.cloned.1.call-update) | async-done | bytes 6291472 | tf_op jit(solution)/shard_map/psum | solution.py:130
  536.1 2.4 multiply_reduce_fusion
  538.7 2.6 collective-permute-start
  541.3 3.5 collective-permute-start.1
  544.9 0.9 tile.93
  545.9 1.1 reshape.166
  548.2 1.2 convolution_bitcast_fusion
  (98 shorter events, 14.3 us)
Async XLA Ops:
  11.4 42.8 %all-to-all-start = ((bf16[64,2,6]{2,1,0:T(2,128)(2,1)}), bf16[64,2,6]{2,1,0:T(2,128)(2,1)S(1)}, u32[]{:S(2)}, u32[]{:S(2)}) async-start(bf16[64,2,6]{2,1,0:T(2,128)(2,1)} %broadcast_select_fusion.1), calls=%async_computation | async-start | bytes 65536 | tf_op jit(solution)/shard_map/all_to_all | solution.py:110
  54.2 10.9 %copy-start = (f32[3,41]{1,0:T(4,128)S(1)}, f32[3,41]{1,0:T(4,128)}, u32[]{:S(2)}) copy-start(f32[3,41]{1,0:T(4,128)} %param.18) | copy-start | bytes 1480
  54.2 12.8 %copy-start.1 = (f32[3,41]{1,0:T(4,128)S(1)}, f32[3,41]{1,0:T(4,128)}, u32[]{:S(2)}) copy-start(f32[3,41]{1,0:T(4,128)} %param.19) | copy-start | bytes 1480
  54.2 251.7 %all-to-all-start.1 = ((bf16[64,2,168,168]{3,2,1,0:T(8,128)(2,1)}), bf16[64,2,168,168]{3,2,1,0:T(8,128)(2,1)}, u32[]{:S(2)}, u32[]{:S(2)}) async-start(bf16[64,2,168,168]{3,2,1,0:T(8,128)(2,1)} %broadcast_select_fusion), calls=%async_computation.1 | async-start | bytes 22020096 | tf_op jit(solution)/shard_map/all_to_all | solution.py:109
  64.9 471.2 %all-reduce.10.cloned.1.call-start = ((), (), s32[]{:S(2)}) async-start(), calls=%async_computation.2 | async-start | bytes 16777216 | tf_op jit(solution)/shard_map/psum | solution.py:130
  374.4 161.7 %copy-start.2 = (f32[6]{0:T(128)S(1)}, f32[6]{0:T(128)}, u32[]{:S(2)}) copy-start(f32[6]{0:T(128)} %param.20) | copy-start | bytes 76
  374.4 170.4 %copy-start.3 = (f32[41]{0:T(128)S(1)}, f32[41]{0:T(128)}, u32[]{:S(2)}) copy-start(f32[41]{0:T(128)} %param.21) | copy-start | bytes 496
  538.7 9.0 %collective-permute-start = (bf16[20,512]{1,0:T(8,128)(2,1)S(1)}, bf16[20,512]{1,0:T(8,128)(2,1)S(1)}, u32[]{:S(2)}, u32[]{:S(2)}) collective-permute-start(bf16[20,512]{1,0:T(8,128)(2,1)S(1)} %bitcast.131), channel_id=1, source_target_pairs={{0,1},{1,2},{2,3},{4,5},{5,6},{6,7},{8,9},{9,10},{10,11},{12,13},{... | collective-permute-start | bytes 61448 | tf_op jit(solution)/shard_map/ppermute | solution.py:17
  541.3 6.9 %collective-permute-start.1 = (bf16[20,512]{0,1:T(8,128)(2,1)S(1)}, bf16[20,512]{0,1:T(8,128)(2,1)S(1)}, u32[]{:S(2)}, u32[]{:S(2)}) collective-permute-start(bf16[20,512]{0,1:T(8,128)(2,1)S(1)} %bitcast.126), channel_id=1, source_target_pairs={{1,0},{2,1},{3,2},{5,4},{6,5},{7,6},{9,8},{10,9},{11,10},{13,12},{... | collective-permute-start | bytes 61448 | tf_op jit(solution)/shard_map/ppermute | solution.py:20
Sparse Core Ops, SparseCore 0:
  374.5 161.5 all-reduce.9
where the time goes:
time: 559 us; the launch traced here: 556 us
  waiting for transfers between devices  390 us (70%)
  local copies, waits for them, and re-layouts  64.9 us (12%)
  matrix products  33.3 us (6%)
  starting transfers between devices  28.9 us (5%)
  other arithmetic  16.9 us (3%)
  between operations  13.9 us (2%)
  blocking collectives  8.51 us (2%)
    all_to_all x1, waiting for transfers between devices, local(): lax.all_to_all(outgoing, 'sky', split_axis=0, concat_axis=0, tiled=True)  236 us
    psum x1, waiting for transfers between devices, local(): full_totals, full_weights = lax.psum((totals, weights), 'band')  153 us
    dot_general x8, matrix products, match_one(): jnp.einsum('kiq,kjq->kij', sectioned, col_kernels, preferred_element_type...  25.1 us
    all_to_all x1, local copies, waits for them, and re-layouts, local(): lax.all_to_all(outgoing, 'sky', split_axis=0, concat_axis=0, tiled=True)  15.3 us
    reshape x2, local copies, waits for them, and re-layouts, local(): raw_blocks.reshape(margin_side, block_count, margin_side).transpose(1, 0, 2)  13.1 us
    all_to_all x1, starting transfers between devices, local(): lax.all_to_all(outgoing_details, 'sky', split_axis=0, concat_axis=0, tile...  11.9 us
  transfers between devices with their start and end apart: 5, of which 3 were waited for; matrix products, arithmetic and copies ran while one was open for 7% of the time, Pallas kernels for 0%

commit v1 on v0

v1 whole, which is shorter than its diff:
```python
import functools

import jax
import jax.numpy as jnp
from jax import lax
from jax.experimental import pallas as pl
from jax.experimental.pallas import tpu as pltpu
from jax.sharding import PartitionSpec as P

B = 128
TAPS = 41
RADIUS = 20
SIDE = 168
NBASIS = 3
BANDS = 6
CR = 4
CC = 4
CELLS = 16
TARGETS = BANDS * CELLS
BLK = 32
CAP = 2
NX, NZ, NC, NY = 4, 8, 2, 4
PLANE = NX * NC * NY
PER_DEST = 2
SLOTS = PER_DEST * CAP
PIECE = 176
MESH = pl.DeviceIdType.MESH
F32 = jnp.float32
BF16 = jnp.bfloat16


def coordinates():
    sky = lax.axis_index("sky")
    core = lax.rem(sky, NC)
    z = lax.rem(lax.div(sky, NC), NZ)
    x = lax.div(sky, NC * NZ)
    return x, z, core, lax.axis_index("band")


def device(x, z, core, y):
    return {"sky": (x * NZ + z) * NC + core, "band": y}


def banded(shape, diagonal, taps, rows):
    distance = diagonal(
        lax.broadcasted_iota(jnp.int32, shape, 0), lax.broadcasted_iota(jnp.int32, shape, 1)
    )

    def step(t, held):
        hit = distance == t
        return tuple(jnp.where(hit, taps(k, t), held[k]) for k in range(rows))

    return lax.fori_loop(0, TAPS, step, tuple(jnp.zeros(shape, F32) for _ in range(rows)))


def match_kernel(
    slot_ref, coef_ref, row_ref, col_ref, raw_ref, out_ref, rowk, colk, sectioned
):
    for part in range(0, B, 32):
        stack = banded((32, 256), lambda i, j: j - i - part, lambda k, t: row_ref[k, t], NBASIS)
        for k in range(NBASIS):
            rowk[k * B + part : k * B + part + 32, :] = stack[k].astype(BF16)
    colk[...] = jnp.zeros_like(colk)
    for part in range(0, 192, 64):
        for shift in range(2):
            stack = banded(
                (64, B),
                lambda u, l: u + part - l - 8 * shift,
                lambda k, t: col_ref[k, t],
                NBASIS,
            )
            for k in range(NBASIS):
                colk[shift, k, B + part : B + part + 64, :] = stack[k].astype(BF16)

    def clear(d, _):
        out_ref[pl.ds(d * SLOTS, SLOTS)] = jnp.zeros((SLOTS, B, B), BF16)
        return 0

    lax.fori_loop(0, PLANE, clear, 0)

    def rows(step, _):
        at = pl.ds(pl.multiple_of(step * 256, 256), 256)
        sectioned[:, at] = jnp.dot(
            rowk[:, :SIDE], raw_ref[:, at], preferred_element_type=F32
        ).astype(BF16)
        return 0

    lax.fori_loop(0, BLK * SIDE // 256, rows, 0)

    def columns(group, _):
        for j in range(16):
            first = j * SIDE // B * B
            offset = j * SIDE - first
            width = 256 if offset + SIDE <= 256 else 384
            shift = offset // 8 % 2
            start = B - offset + 8 * shift
            at = pl.ds(pl.multiple_of(group * (16 * SIDE) + first, B), width)
            block = group * 16 + j
            total = None
            for k in range(NBASIS):
                term = coef_ref[block, k] * jnp.dot(
                    sectioned[k * B : (k + 1) * B, at],
                    colk[shift, k, start : start + width, :],
                    preferred_element_type=F32,
                )
                total = term if total is None else total + term
            out_ref[slot_ref[block]] = total.astype(BF16)
        return 0

    lax.fori_loop(0, BLK // 16, columns, 0)


def match(slot, coef, row_basis, col_basis, raw):
    smem = pl.BlockSpec(memory_space=pltpu.SMEM)
    vmem = pl.BlockSpec(memory_space=pltpu.VMEM)
    return pl.pallas_call(
        match_kernel,
        out_shape=jax.ShapeDtypeStruct((PLANE * SLOTS, B, B), BF16),
        in_specs=[smem, smem, smem, smem, vmem],
        out_specs=vmem,
        scratch_shapes=[
            pltpu.VMEM((NBASIS * B, 256), BF16),
            pltpu.VMEM((2, NBASIS, 512, B), BF16),
            pltpu.VMEM((NBASIS * B, BLK * SIDE), BF16),
        ],
        compiler_params=pltpu.CompilerParams(vmem_limit_bytes=48 * 1024 * 1024),
        name="match",
    )(slot, coef, row_basis, col_basis, raw)


def plane_device(index, z):
    return device(
        lax.div(index, NC * NY), z, lax.rem(lax.div(index, NY), NC), lax.rem(index, NY)
    )


def plane_kernel(out_ref, in_ref, own, send_sem, recv_sem, own_sem):
    x, z, core, y = coordinates()
    me = (x * NC + core) * NY + y
    barrier = pltpu.get_barrier_semaphore()
    for step in range(1, PLANE):
        pl.semaphore_signal(
            barrier,
            inc=1,
            device_id=plane_device(lax.rem(me + step, PLANE), z),
            device_id_type=MESH,
        )
    take = pltpu.make_async_copy(out_ref.at[me], own, own_sem)
    take.start()
    pl.semaphore_wait(barrier, PLANE - 1)
    copies = []
    for step in range(1, PLANE):
        peer = lax.rem(me + step, PLANE)
        copy = pltpu.make_async_remote_copy(
            src_ref=out_ref.at[peer],
            dst_ref=in_ref.at[me],
            send_sem=send_sem.at[step],
            recv_sem=recv_sem.at[step],
            device_id=plane_device(peer, z),
            device_id_type=MESH,
        )
        copy.start()
        copies.append(copy)
    take.wait()
    put = pltpu.make_async_copy(own, in_ref.at[me], own_sem)
    put.start()
    put.wait()
    for copy in copies:
        copy.wait()


def plane_exchange(outgoing):
    hbm = pl.BlockSpec(memory_space=pl.ANY)
    return pl.pallas_call(
        plane_kernel,
        out_shape=jax.ShapeDtypeStruct((PLANE, SLOTS, B, B), BF16),
        in_specs=[hbm],
        out_specs=hbm,
        scratch_shapes=[
            pltpu.VMEM((SLOTS, B, B), BF16),
            pltpu.SemaphoreType.DMA((PLANE,)),
            pltpu.SemaphoreType.DMA((PLANE,)),
            pltpu.SemaphoreType.DMA,
        ],
        compiler_params=pltpu.CompilerParams(collective_id=0, has_side_effects=True),
        name="plane_exchange",
    )(outgoing)


def gather_kernel(cell_ref, scale_ref, in_ref, out_ref, total):
    step = pl.program_id(0)
    per_step = in_ref.shape[0]

    @pl.when(step == 0)
    def _():
        def clear(i, _):
            total[pl.ds(pl.multiple_of(i * 64, 64), 64), :] = jnp.zeros((64, CC * B), F32)
            return 0

        lax.fori_loop(0, PER_DEST * CR * B // 64, clear, 0)

    for d in range(per_step):
        for s in range(SLOTS):
            slot = (step * per_step + d) * SLOTS + s
            cell = cell_ref[slot]

            @pl.when(cell >= 0)
            def _():
                row = pl.multiple_of((s // CAP) * (CR * B) + lax.div(cell, CC) * B, B)
                column = pl.multiple_of(lax.rem(cell, CC) * B, B)
                total[pl.ds(row, B), pl.ds(column, B)] += scale_ref[slot] * in_ref[d, s].astype(F32)

    @pl.when(step == pl.num_programs(0) - 1)
    def _():
        for q in range(PER_DEST):
            base = q * CR * B
            for r in range(CR):
                low, high = r * B - RADIUS, (r + 1) * B + RADIUS
                parts = []
                if low < 0:
                    parts.append(jnp.zeros((RADIUS, CC * B), F32))
                parts.append(total[base + max(low, 0) : base + min(high, CR * B), :])
                if high > CR * B:
                    parts.append(jnp.zeros((RADIUS, CC * B), F32))
                parts.append(jnp.zeros((PIECE - SIDE, CC * B), F32))
                out_ref[q * CR + r] = jnp.concatenate(parts, axis=0).astype(BF16)


def gather_slots(cell, scale, arrived):
    smem = pl.BlockSpec(memory_space=pltpu.SMEM)
    per_step = 4
    return pl.pallas_call(
        gather_kernel,
        grid=(PLANE // per_step,),
        out_shape=jax.ShapeDtypeStruct((PER_DEST * CR, PIECE, CC * B), BF16),
        in_specs=[smem, smem, pl.BlockSpec((per_step, SLOTS, B, B), lambda i: (i, 0, 0, 0))],
        out_specs=pl.BlockSpec((PER_DEST * CR, PIECE, CC * B), lambda i: (0, 0, 0)),
        scratch_shapes=[pltpu.VMEM((PER_DEST * CR * B, CC * B), F32)],
        compiler_params=pltpu.CompilerParams(vmem_limit_bytes=48 * 1024 * 1024),
        name="gather_slots",
    )(cell, scale, arrived)


def detect_kernel(
    taps_ref, piece_ref, out_ref, held, rowf, colf, padded, send_sem, recv_sem, own_sem
):
    x, z, core, y = coordinates()
    barrier = pltpu.get_barrier_semaphore()
    me = z * NY + y
    for step in range(1, NZ * NY):
        other = lax.rem(me + step, NZ * NY)
        pl.semaphore_signal(
            barrier,
            inc=1,
            device_id=device(x, lax.div(other, NY), core, lax.rem(other, NY)),
            device_id_type=MESH,
        )
    pl.semaphore_wait(barrier, NZ * NY - 1)

    def outgoing(q, r):
        return pltpu.make_async_remote_copy(
            src_ref=piece_ref.at[q * CR + r],
            dst_ref=held.at[z],
            send_sem=send_sem.at[q * CR + r],
            recv_sem=recv_sem.at[z],
            device_id=device(x, PER_DEST * y + q, core, r),
            device_id_type=MESH,
        )

    def is_own(q, r):
        return (z == PER_DEST * y + q) & (r == y)

    for q in range(PER_DEST):
        for r in range(CR):

            @pl.when(jnp.logical_not(is_own(q, r)))
            def _():
                outgoing(q, r).start()

            @pl.when(is_own(q, r))
            def _():
                pltpu.make_async_copy(piece_ref.at[q * CR + r], held.at[z], own_sem).start()

    def tap(k, t):
        return taps_ref[t]

    for part in range(0, B, 32):
        rowf[part : part + 32, :] = banded((32, 256), lambda i, j: j - i - part, tap, 1)[0].astype(
            BF16
        )
    for part in range(0, 384, 64):
        colf[part : part + 64, :] = banded(
            (64, B), lambda m, l: m + part - B - l + RADIUS, tap, 1
        )[0].astype(BF16)
    padded[:, :B] = jnp.zeros((B, B), BF16)
    padded[:, B + CC * B :] = jnp.zeros((B, B), BF16)

    own_here = y == lax.div(z, PER_DEST)
    for source in range(NZ):
        mine = own_here & (z == source)

        @pl.when(jnp.logical_not(mine))
        def _():
            pltpu.make_async_remote_copy(
                src_ref=piece_ref.at[0],
                dst_ref=held.at[source],
                send_sem=send_sem.at[0],
                recv_sem=recv_sem.at[source],
                device_id=device(x, source, core, lax.div(z, PER_DEST)),
                device_id_type=MESH,
            ).wait_recv()

        @pl.when(mine)
        def _():
            pltpu.make_async_copy(piece_ref.at[0], held.at[source], own_sem).wait()

    for c in range(CC):
        at = slice(c * B, (c + 1) * B)
        combined = held[0, :, at].astype(F32)
        for source in range(1, NZ):
            combined = combined + held[source, :, at].astype(F32)
        padded[:, B + c * B : 2 * B + c * B] = jnp.dot(
            rowf[:, :PIECE], combined.astype(BF16), preferred_element_type=F32
        ).astype(BF16)
    for c in range(CC):
        out_ref[:, c * B : (c + 1) * B] = jnp.dot(
            padded[:, c * B : c * B + 384], colf[...], preferred_element_type=F32
        )
    for q in range(PER_DEST):
        for r in range(CR):

            @pl.when(jnp.logical_not(is_own(q, r)))
            def _():
                outgoing(q, r).wait_send()


def detect(taps, pieces):
    return pl.pallas_call(
        detect_kernel,
        out_shape=jax.ShapeDtypeStruct((B, CC * B), F32),
        in_specs=[pl.BlockSpec(memory_space=pltpu.SMEM), pl.BlockSpec(memory_space=pl.ANY)],
        out_specs=pl.BlockSpec(memory_space=pltpu.VMEM),
        scratch_shapes=[
            pltpu.VMEM((NZ, PIECE, CC * B), BF16),
            pltpu.VMEM((B, 256), BF16),
            pltpu.VMEM((384, B), BF16),
            pltpu.VMEM((B, (CC + 2) * B), BF16),
            pltpu.SemaphoreType.DMA((PER_DEST * CR,)),
            pltpu.SemaphoreType.DMA((NZ,)),
            pltpu.SemaphoreType.DMA,
        ],
        compiler_params=pltpu.CompilerParams(collective_id=1, has_side_effects=True),
        name="detect",
    )(taps, pieces)


def ranks(patch):
    earlier = jnp.arange(BLK)[None, :] < jnp.arange(BLK)[:, None]
    same = patch[..., :, None] == patch[..., None, :]
    return jnp.sum((same & earlier).astype(jnp.int32), axis=-1)


def local(
    raw_blocks,
    patch_of_block,
    cell_of_block,
    band_of_block,
    block_weight,
    basis_coef,
    row_basis,
    col_basis,
    band_gain,
    filter_taps,
):
    x, z, core, y = coordinates()
    patch = patch_of_block[:, 0]
    own_details = jnp.stack(
        [v.astype(F32) for v in (patch, cell_of_block, band_of_block, block_weight)]
    )
    details = lax.all_gather(own_details, ("sky", "band"), axis=0, tiled=False)
    names = details[:, :3].astype(jnp.int32)
    weights = details[:, 3]

    patch_core = patch % NC
    patch_z = patch // NC % NZ
    patch_x = patch // (NC * NZ)
    dest = (patch_x * NC + patch_core) * NY + patch_z // PER_DEST
    slot = dest * SLOTS + (patch_z % PER_DEST) * CAP + ranks(patch)
    outgoing = match(slot, basis_coef.astype(F32), row_basis, col_basis, raw_blocks)
    arrived = plane_exchange(outgoing.reshape(PLANE, SLOTS, B, B))

    first_patch = (x * NZ + PER_DEST * y) * NC + core
    my_patches = first_patch + NC * jnp.arange(PER_DEST, dtype=jnp.int32)
    every_key = (names[:, 0] * TARGETS + names[:, 2] * CELLS + names[:, 1]).reshape(-1)
    every_weight = weights.reshape(-1)
    bins = (my_patches[:, None] * TARGETS + jnp.arange(TARGETS, dtype=jnp.int32)).reshape(-1)
    weight_sum = jnp.sum(
        jnp.where(every_key[None, :] == bins[:, None], every_weight[None, :], 0.0), axis=1
    )
    gain = jnp.tile(jnp.repeat(band_gain, CELLS), PER_DEST) / jnp.maximum(weight_sum, 1.0)
    near = lax.dynamic_index_in_dim(
        details.reshape(NX, NZ, NC * NY, 4, BLK), z, axis=1, keepdims=False
    ).reshape(PLANE, 4, BLK)
    near_names = near[:, :3].astype(jnp.int32)
    near_patch, near_cell = near_names[:, 0], near_names[:, 1]
    near_key = near_patch * TARGETS + near_names[:, 2] * CELLS + near_cell
    near_gain = jnp.sum(jnp.where(near_key[..., None] == bins, gain, 0.0), axis=-1)
    near_scale = near_gain * near[:, 3]
    near_rank = ranks(near_patch)
    chosen = (near_patch[:, None, None, :] == my_patches[:, None, None]) & (
        near_rank[:, None, None, :] == jnp.arange(CAP, dtype=jnp.int32)[:, None]
    )
    scale = jnp.sum(jnp.where(chosen, near_scale[:, None, None, :], 0.0), axis=-1).reshape(-1)
    cell = jnp.sum(jnp.where(chosen, near_cell[:, None, None, :] + 1, 0), axis=-1).reshape(-1) - 1

    pieces = gather_slots(cell, scale, arrived)
    taps = filter_taps.astype(BF16).astype(F32)
    return detect(taps, pieces)[None]


def solution(mesh):
    return jax.shard_map(
        local,
        mesh=mesh,
        in_specs=(
            P(None, ("sky", "band")),
            P(("sky", "band"), None),
            P(("sky", "band")),
            P(("sky", "band")),
            P(("sky", "band")),
            P(("sky", "band"), None),
            P(),
            P(),
            P(),
            P(),
        ),
        out_specs=P("sky", "band", None),
        check_vma=False,
    )
```

time: 559 us -> 340 us (0.61)
  the two profiles are of different devices: /device:TPU:16 before, /device:TPU:56 now
where the time goes in v1:
time: 340 us; the launch traced here: 339 us
  Pallas kernels  208 us (61%)
  blocking collectives  117 us (34%)
  local copies, waits for them, and re-layouts  8.46 us (2%)
  other arithmetic  6.06 us (2%)
    pallas_call x1, Pallas kernels, detect(): pl.pallas_call(detect_kernel, out_shape=jax.ShapeDtypeStruct((B, CC * B),...  123 us
    all_gather x1, blocking collectives, local(): details = lax.all_gather(own_details, ('sky', 'band'), axis=0, tiled=False)  117 us
    pallas_call x1, Pallas kernels, plane_exchange(): pl.pallas_call(plane_kernel, out_shape=jax.ShapeDtypeStruct((PLANE, SLOTS...  69.1 us
    pallas_call x1, Pallas kernels, match(): pl.pallas_call(match_kernel, out_shape=jax.ShapeDtypeStruct((PLANE * SLOT...  12.6 us
    unnamed x21, local copies, waits for them, and re-layouts  6.91 us

profile of v1, /device:TPU:56, one launch (start us, length us, event | category | flops | bytes accessed | tf_op | source)
XLA Modules:
  0.0 339.4 jit_solution(5775689095311831114)
XLA Ops:
  0.1 0.8 convert_bitcast_fusion
  0.9 0.7 bitcast_convert_fusion
  1.5 0.7 convert_bitcast_fusion.2
  2.2 117.0 %all-gather.1 = f32[256,4,32]{2,1,0:T(4,128)S(1)} all-gather(f32[1,4,32]{2,1,0:T(4,128)S(1)} %maximum_bitcast_fusion), channel_id=2, replica_groups=mesh['sky'=64,'band'=4] {'sky','band'}, dimensions={0}, use_global_device_ids=true | all-gather | bytes 131584 | tf_op jit(solution)/shard_map/all_gather | solution.py:380
  119.4 0.1 add.134
  119.5 0.1 slice_convert_fusion
  119.5 0.6 fusion
  120.1 0.1 add.137
  120.2 0.4 slice_reduce_fusion
  120.6 0.1 broadcast_in_dim.65
  120.7 0.9 select_reduce_fusion
  121.7 0.1 tile.10
  121.8 0.1 tile.12
  121.9 0.4 select_reduce_fusion.1
  122.4 0.8 convert_reduce_fusion
  123.2 0.1 fusion.3
  123.3 0.1 copy.25
  123.4 0.2 reshape.153.scale_ref
  123.6 0.2 fusion.2
  123.7 0.1 copy.24
  123.8 0.1 sub.21.cell_ref
  124.0 0.1 copy.26.coef_ref
  124.1 0.2 convert_reduce_fusion.1
  124.3 12.6 %match.1 = bf16[128,128,128]{2,1,0:T(8,128)(2,1)S(1)} custom-call(s32[32]{0:T(128)S(1)} %fusion.12.slot_ref, f32[32,3]{1,0:T(8,128)S(1)} %copy.26.coef_ref, f32[3,41]{1,0:T(4,128)S(1)} %copy-done.4, f32[3,41]{1,0:T(4,128)S(1)} %copy-done.5, bf16[168,5376]{1,0:T(8,128)(2,1)S(1)} %copy-done.3), custom_call_target="tpu_custom_call" | custom-call | tf_op jit(solution)/shard_map/match/pallas_call | solution.py:116
  137.0 1.9 copy-done.1
  138.9 69.1 %plane_exchange.1.in_ref = bf16[32,4,128,128]{3,2,1,0:T(8,128)(2,1)} custom-call(bf16[32,4,128,128]{3,2,1,0:T(8,128)(2,1)} %bitcast.38), custom_call_target="tpu_custom_call" | custom-call | tf_op jit(solution)/shard_map/plane_exchange/pallas_call | solution.py:174
  208.1 2.2 copy-done
  210.2 2.5 gather_slots.1.piece_ref
  212.7 1.1 copy-done.2
  213.8 0.5 convert_convert_fusion.taps_ref
  214.3 123.4 %detect.1 = f32[128,512]{1,0:T(8,128)} custom-call(f32[41]{0:T(128)} %convert_convert_fusion.taps_ref, bf16[8,176,512]{2,1,0:T(8,128)(2,1)} %copy-done.2), custom_call_target="tpu_custom_call" | custom-call | tf_op jit(solution)/shard_map/detect/pallas_call | solution.py:338
  337.7 1.7 copy.28
  (34 shorter events, 0.4 us)
Async XLA Ops:
  0.0 124.1 %copy-start.8 = (s32[32,1]{0,1:T(1,128)S(1)}, s32[32,1]{0,1:T(1,128)}, u32[]{:S(2)}) copy-start(s32[32,1]{0,1:T(1,128)} %param.11) | copy-start | bytes 388
  0.0 121.6 %copy-start.7 = (f32[6]{0:T(128)S(1)}, f32[6]{0:T(128)}, u32[]{:S(2)}) copy-start(f32[6]{0:T(128)} %param.18) | copy-start | bytes 76
  0.0 124.0 %copy-start.6 = (bf16[32,3]{0,1:T(4,128)(2,1)S(1)}, bf16[32,3]{0,1:T(4,128)(2,1)}, u32[]{:S(2)}) copy-start(bf16[32,3]{0,1:T(4,128)(2,1)} %param.15) | copy-start | bytes 580
  0.0 124.3 %copy-start.3 = (bf16[168,5376]{1,0:T(8,128)(2,1)S(1)}, bf16[168,5376]{1,0:T(8,128)(2,1)}, u32[]{:S(2)}) copy-start(bf16[168,5376]{1,0:T(8,128)(2,1)} %raw_ref.1) | copy-start | bytes 5419012
  0.0 124.3 %copy-start.4 = (f32[3,41]{1,0:T(4,128)S(1)}, f32[3,41]{1,0:T(4,128)}, u32[]{:S(2)}) copy-start(f32[3,41]{1,0:T(4,128)} %row_ref.1) | copy-start | bytes 1480
  0.0 124.3 %copy-start.5 = (f32[3,41]{1,0:T(4,128)S(1)}, f32[3,41]{1,0:T(4,128)}, u32[]{:S(2)}) copy-start(f32[3,41]{1,0:T(4,128)} %col_ref.1) | copy-start | bytes 1480
  137.0 1.9 copy-start.1
  208.1 2.2 copy-start
  210.2 3.6 %copy-start.9 = (f32[41]{0:T(128)S(1)}, f32[41]{0:T(128)}, u32[]{:S(2)}) copy-start(f32[41]{0:T(128)} %param.19) | copy-start | bytes 496
  212.7 1.1 copy-start.2

commit v2 on v1

v2 whole, which is shorter than its diff:
```python
import functools

import jax
import jax.numpy as jnp
from jax import lax
from jax.experimental import pallas as pl
from jax.experimental.pallas import tpu as pltpu
from jax.sharding import PartitionSpec as P

B = 128
TAPS = 41
RADIUS = 20
SIDE = 168
NBASIS = 3
BANDS = 6
CR = 4
CC = 4
CELLS = 16
TARGETS = BANDS * CELLS
BLK = 32
CAP = 2
NX, NZ, NC, NY = 4, 8, 2, 4
PLANE = NX * NC * NY
SLOTS = NZ * CAP
STRIP = B // NY
ROWS = B + 2 * STRIP
MESH = pl.DeviceIdType.MESH
F32 = jnp.float32
BF16 = jnp.bfloat16


def coordinates():
    sky = lax.axis_index("sky")
    core = lax.rem(sky, NC)
    z = lax.rem(lax.div(sky, NC), NZ)
    x = lax.div(sky, NC * NZ)
    return x, z, core, lax.axis_index("band")


def device(x, z, core, y):
    return {"sky": (x * NZ + z) * NC + core, "band": y}


def banded(shape, diagonal, taps, rows):
    distance = diagonal(
        lax.broadcasted_iota(jnp.int32, shape, 0), lax.broadcasted_iota(jnp.int32, shape, 1)
    )

    def step(t, held):
        hit = distance == t
        return tuple(jnp.where(hit, taps(k, t), held[k]) for k in range(rows))

    return lax.fori_loop(0, TAPS, step, tuple(jnp.zeros(shape, F32) for _ in range(rows)))


def match_kernel(
    slot_ref, coef_ref, row_ref, col_ref, raw_ref, out_ref, rowk, colk, sectioned
):
    for part in range(0, B, 32):
        stack = banded((32, 256), lambda i, j: j - i - part, lambda k, t: row_ref[k, t], NBASIS)
        for k in range(NBASIS):
            rowk[k * B + part : k * B + part + 32, :] = stack[k].astype(BF16)
    colk[...] = jnp.zeros_like(colk)
    for part in range(0, 192, 64):
        for shift in range(2):
            stack = banded(
                (64, B),
                lambda u, l: u + part - l - 8 * shift,
                lambda k, t: col_ref[k, t],
                NBASIS,
            )
            for k in range(NBASIS):
                colk[shift, k, B + part : B + part + 64, :] = stack[k].astype(BF16)

    def clear(d, _):
        out_ref[pl.ds(d * SLOTS, SLOTS)] = jnp.zeros((SLOTS, STRIP, B), BF16)
        return 0

    lax.fori_loop(0, PLANE, clear, 0)

    def rows(step, _):
        at = pl.ds(pl.multiple_of(step * 256, 256), 256)
        sectioned[:, at] = jnp.dot(
            rowk[:, :SIDE], raw_ref[:, at], preferred_element_type=F32
        ).astype(BF16)
        return 0

    lax.fori_loop(0, BLK * SIDE // 256, rows, 0)

    def columns(group, _):
        for j in range(16):
            first = j * SIDE // B * B
            offset = j * SIDE - first
            width = 256 if offset + SIDE <= 256 else 384
            shift = offset // 8 % 2
            start = B - offset + 8 * shift
            at = pl.ds(pl.multiple_of(group * (16 * SIDE) + first, B), width)
            block = group * 16 + j
            total = None
            for k in range(NBASIS):
                term = coef_ref[block, k] * jnp.dot(
                    sectioned[k * B : (k + 1) * B, at],
                    colk[shift, k, start : start + width, :],
                    preferred_element_type=F32,
                )
                total = term if total is None else total + term
            slot = slot_ref[block]
            for strip in range(NY):
                out_ref[slot + strip * SLOTS] = total[strip * STRIP : (strip + 1) * STRIP].astype(
                    BF16
                )
        return 0

    lax.fori_loop(0, BLK // 16, columns, 0)


def match(slot, coef, row_basis, col_basis, raw):
    smem = pl.BlockSpec(memory_space=pltpu.SMEM)
    vmem = pl.BlockSpec(memory_space=pltpu.VMEM)
    return pl.pallas_call(
        match_kernel,
        out_shape=jax.ShapeDtypeStruct((PLANE * SLOTS, STRIP, B), BF16),
        in_specs=[smem, smem, smem, smem, vmem],
        out_specs=vmem,
        scratch_shapes=[
            pltpu.VMEM((NBASIS * B, 256), BF16),
            pltpu.VMEM((2, NBASIS, 512, B), BF16),
            pltpu.VMEM((NBASIS * B, BLK * SIDE), BF16),
        ],
        compiler_params=pltpu.CompilerParams(vmem_limit_bytes=24 * 1024 * 1024),
        name="match",
    )(slot, coef, row_basis, col_basis, raw)


def plane_device(index, z):
    return device(
        lax.div(index, NC * NY), z, lax.rem(lax.div(index, NY), NC), lax.rem(index, NY)
    )


def plane_kernel(
    out_ref,
    info_ref,
    in_ref,
    every_ref,
    own,
    send_sem,
    recv_sem,
    info_send,
    info_recv,
    z_send,
    z_recv,
    own_sem,
    info_sem,
):
    x, z, core, y = coordinates()
    me = (x * NC + core) * NY + y
    barrier = pltpu.get_barrier_semaphore()
    for step in range(1, PLANE):
        pl.semaphore_signal(
            barrier,
            inc=1,
            device_id=plane_device(lax.rem(me + step, PLANE), z),
            device_id_type=MESH,
        )
    for step in range(1, NZ):
        pl.semaphore_signal(
            barrier,
            inc=1,
            device_id=device(x, lax.rem(z + step, NZ), core, y),
            device_id_type=MESH,
        )
    take = pltpu.make_async_copy(out_ref.at[me], own, own_sem)
    take.start()
    keep = pltpu.make_async_copy(info_ref.at[0], every_ref.at[z, me], info_sem)
    keep.start()
    pl.semaphore_wait(barrier, PLANE - 1 + NZ - 1)
    infos = []
    for step in range(1, PLANE):
        copy = pltpu.make_async_remote_copy(
            src_ref=info_ref.at[0],
            dst_ref=every_ref.at[z, me],
            send_sem=info_send.at[step],
            recv_sem=info_recv.at[step],
            device_id=plane_device(lax.rem(me + step, PLANE), z),
            device_id_type=MESH,
        )
        copy.start()
        infos.append(copy)
    copies = []
    for step in range(1, PLANE):
        peer = lax.rem(me + step, PLANE)
        copy = pltpu.make_async_remote_copy(
            src_ref=out_ref.at[peer],
            dst_ref=in_ref.at[me],
            send_sem=send_sem.at[step],
            recv_sem=recv_sem.at[step],
            device_id=plane_device(peer, z),
            device_id_type=MESH,
        )
        copy.start()
        copies.append(copy)
    take.wait()
    put = pltpu.make_async_copy(own, in_ref.at[me], own_sem)
    put.start()
    keep.wait()
    for copy in infos:
        copy.wait()
    planes = []
    for step in range(1, NZ):
        copy = pltpu.make_async_remote_copy(
            src_ref=every_ref.at[z],
            dst_ref=every_ref.at[z],
            send_sem=z_send.at[step],
            recv_sem=z_recv.at[step],
            device_id=device(x, lax.rem(z + step, NZ), core, y),
            device_id_type=MESH,
        )
        copy.start()
        planes.append(copy)
    put.wait()
    for copy in planes:
        copy.wait()
    for copy in copies:
        copy.wait()


def plane_exchange(outgoing, info):
    hbm = pl.BlockSpec(memory_space=pl.ANY)
    vmem = pl.BlockSpec(memory_space=pltpu.VMEM)
    dma = pltpu.SemaphoreType.DMA
    return pl.pallas_call(
        plane_kernel,
        out_shape=(
            jax.ShapeDtypeStruct((PLANE, SLOTS, STRIP, B), BF16),
            jax.ShapeDtypeStruct((NZ, PLANE, 1, B), F32),
        ),
        in_specs=[hbm, vmem],
        out_specs=(hbm, vmem),
        scratch_shapes=[
            pltpu.VMEM((SLOTS, STRIP, B), BF16),
            dma((PLANE,)),
            dma((PLANE,)),
            dma((PLANE,)),
            dma((PLANE,)),
            dma((NZ,)),
            dma((NZ,)),
            dma,
            dma,
        ],
        compiler_params=pltpu.CompilerParams(
            collective_id=0, has_side_effects=True, vmem_limit_bytes=4 * 1024 * 1024
        ),
        name="plane_exchange",
    )(outgoing, info)


def gather_kernel(cell_ref, scale_ref, in_ref, out_ref, total):
    step = pl.program_id(0)
    per_step = in_ref.shape[0]

    @pl.when(step == 0)
    def _():
        def clear(i, _):
            total[i] = jnp.zeros((STRIP, CC * B), F32)
            return 0

        lax.fori_loop(0, NZ * CR, clear, 0)

    for d in range(per_step):
        for s in range(SLOTS):
            slot = (step * per_step + d) * SLOTS + s
            cell = cell_ref[slot]

            @pl.when(cell >= 0)
            def _():
                row = (s // CAP) * CR + lax.div(cell, CC)
                column = pl.multiple_of(lax.rem(cell, CC) * B, B)
                total[row, :, pl.ds(column, B)] += scale_ref[slot] * in_ref[d, s].astype(F32)

    @pl.when(step == pl.num_programs(0) - 1)
    def _():
        def write(i, _):
            out_ref[i] = total[i].astype(BF16)
            return 0

        lax.fori_loop(0, NZ * CR, write, 0)


def gather_slots(cell, scale, arrived):
    smem = pl.BlockSpec(memory_space=pltpu.SMEM)
    per_step = 4
    shape = (NZ * CR, STRIP, CC * B)
    return pl.pallas_call(
        gather_kernel,
        grid=(PLANE // per_step,),
        out_shape=jax.ShapeDtypeStruct(shape, BF16),
        in_specs=[smem, smem, pl.BlockSpec((per_step, SLOTS, STRIP, B), lambda i: (i, 0, 0, 0))],
        out_specs=pl.BlockSpec(shape, lambda i: (0, 0, 0)),
        scratch_shapes=[pltpu.VMEM(shape, F32)],
        compiler_params=pltpu.CompilerParams(vmem_limit_bytes=16 * 1024 * 1024),
        name="gather_slots",
    )(cell, scale, arrived)


def detect_kernel(
    taps_ref,
    piece_ref,
    out_ref,
    held,
    strips,
    window,
    rowf,
    colf,
    padded,
    z_send,
    z_recv,
    y_send,
    y_recv,
    edge_send,
    edge_recv,
    own_sem,
):
    x, z, core, y = coordinates()
    barrier = pltpu.get_barrier_semaphore()
    for step in range(1, NZ):
        pl.semaphore_signal(
            barrier,
            inc=1,
            device_id=device(x, lax.rem(z + step, NZ), core, y),
            device_id_type=MESH,
        )
    for step in range(1, NY):
        pl.semaphore_signal(
            barrier,
            inc=1,
            device_id=device(x, z, core, lax.rem(y + step, NY)),
            device_id_type=MESH,
        )
    keep = pltpu.make_async_copy(piece_ref.at[z], held.at[z], own_sem)
    keep.start()
    pl.semaphore_wait(barrier, NZ - 1 + NY - 1)
    pieces = []
    for step in (4, 3, 5, 2, 6, 1, 7):
        peer = lax.rem(z + step, NZ)
        copy = pltpu.make_async_remote_copy(
            src_ref=piece_ref.at[peer],
            dst_ref=held.at[z],
            send_sem=z_send.at[step],
            recv_sem=z_recv.at[step],
            device_id=device(x, peer, core, y),
            device_id_type=MESH,
        )
        copy.start()
        pieces.append(copy)

    def tap(k, t):
        return taps_ref[t]

    for part in range(0, B, 32):
        rowf[part : part + 32, :] = banded(
            (32, 256), lambda i, u: u - i - part - (STRIP - RADIUS), tap, 1
        )[0].astype(BF16)
    for part in range(0, 384, 64):
        colf[part : part + 64, :] = banded(
            (64, B), lambda m, l: m + part - B - l + RADIUS, tap, 1
        )[0].astype(BF16)
    padded[:, :B] = jnp.zeros((B, B), BF16)
    padded[:, B + CC * B :] = jnp.zeros((B, B), BF16)

    keep.wait()
    for copy in pieces:
        copy.wait()
    for r in range(CR):
        combined = held[0, r].astype(F32)
        for source in range(1, NZ):
            combined = combined + held[source, r].astype(F32)
        strips[r] = combined.astype(BF16)

    sends = []
    for step in range(1, NY):
        r = lax.rem(y + step, NY)
        copy = pltpu.make_async_remote_copy(
            src_ref=strips.at[r],
            dst_ref=window.at[1 + y],
            send_sem=y_send.at[step],
            recv_sem=y_recv.at[step],
            device_id=device(x, z, core, r),
            device_id_type=MESH,
        )
        copy.start()
        sends.append(copy)

    def edge(r, upper):
        return pltpu.make_async_remote_copy(
            src_ref=strips.at[r - 1 if upper else r + 1],
            dst_ref=window.at[0 if upper else NY + 1],
            send_sem=edge_send.at[r],
            recv_sem=edge_recv.at[0 if upper else 1],
            device_id=device(x, z, core, r),
            device_id_type=MESH,
        )

    @pl.when(y == NY - 1)
    def _():
        for r in range(1, NY - 1):
            edge(r, True).start()
        window[0] = strips[NY - 2]
        window[NY + 1] = jnp.zeros((STRIP, CC * B), BF16)

    @pl.when(y == 0)
    def _():
        for r in range(1, NY - 1):
            edge(r, False).start()
        window[0] = jnp.zeros((STRIP, CC * B), BF16)
        window[NY + 1] = strips[1]

    window[1 + y] = strips[y]
    for copy in sends:
        copy.wait()

    @pl.when((y > 0) & (y < NY - 1))
    def _():
        edge(1, True).wait_recv()
        edge(1, False).wait_recv()

    @pl.when(y == NY - 1)
    def _():
        for r in range(1, NY - 1):
            edge(r, True).wait_send()

    @pl.when(y == 0)
    def _():
        for r in range(1, NY - 1):
            edge(r, False).wait_send()

    for c in range(CC):
        at = slice(c * B, (c + 1) * B)
        padded[:, B + c * B : 2 * B + c * B] = jnp.dot(
            rowf[:, :ROWS], window[:, :, at].reshape(ROWS, B), preferred_element_type=F32
        ).astype(BF16)
    for c in range(CC):
        out_ref[:, c * B : (c + 1) * B] = jnp.dot(
            padded[:, c * B : c * B + 384], colf[...], preferred_element_type=F32
        )


def detect(taps, pieces):
    dma = pltpu.SemaphoreType.DMA
    return pl.pallas_call(
        detect_kernel,
        out_shape=jax.ShapeDtypeStruct((B, CC * B), F32),
        in_specs=[pl.BlockSpec(memory_space=pltpu.SMEM), pl.BlockSpec(memory_space=pl.ANY)],
        out_specs=pl.BlockSpec(memory_space=pltpu.VMEM),
        scratch_shapes=[
            pltpu.VMEM((NZ, CR, STRIP, CC * B), BF16),
            pltpu.VMEM((CR, STRIP, CC * B), BF16),
            pltpu.VMEM((NY + 2, STRIP, CC * B), BF16),
            pltpu.VMEM((B, 256), BF16),
            pltpu.VMEM((384, B), BF16),
            pltpu.VMEM((B, (CC + 2) * B), BF16),
            dma((NZ,)),
            dma((NZ,)),
            dma((NY,)),
            dma((NY,)),
            dma((NY,)),
            dma((2,)),
            dma,
        ],
        compiler_params=pltpu.CompilerParams(
            collective_id=1, has_side_effects=True, vmem_limit_bytes=8 * 1024 * 1024
        ),
        name="detect",
    )(taps, pieces)


def ranks(patch):
    earlier = jnp.arange(BLK)[None, :] < jnp.arange(BLK)[:, None]
    same = patch[..., :, None] == patch[..., None, :]
    return jnp.sum((same & earlier).astype(jnp.int32), axis=-1)


def local(
    raw_blocks,
    patch_of_block,
    cell_of_block,
    band_of_block,
    block_weight,
    basis_coef,
    row_basis,
    col_basis,
    band_gain,
    filter_taps,
):
    x, z, core, y = coordinates()
    patch = patch_of_block[:, 0]
    own_details = jnp.stack(
        [v.astype(F32) for v in (patch, cell_of_block, band_of_block, block_weight)]
    )
    patch_core = patch % NC
    patch_z = patch // NC % NZ
    patch_x = patch // (NC * NZ)
    slot = (patch_x * NC + patch_core) * (NY * SLOTS) + patch_z * CAP + ranks(patch)
    outgoing = match(slot, basis_coef.astype(F32), row_basis, col_basis, raw_blocks)
    arrived, details = plane_exchange(
        outgoing.reshape(PLANE, SLOTS, STRIP, B), own_details.reshape(1, 1, 4 * BLK)
    )
    details = details.reshape(NZ, PLANE, 4, BLK)

    my_patches = (x * NZ + jnp.arange(NZ, dtype=jnp.int32)) * NC + core
    every_patch = details[:, :, 0].astype(jnp.int32).reshape(-1)
    every_target = (details[:, :, 2] * CELLS + details[:, :, 1]).astype(jnp.int32).reshape(-1)
    every_weight = details[:, :, 3].reshape(-1)
    share = jnp.where(every_patch == my_patches[:, None], every_weight, 0.0).astype(BF16)
    hits = (every_target == jnp.arange(TARGETS, dtype=jnp.int32)[:, None]).astype(BF16)
    weight_sum = lax.dot_general(
        share, hits, (((1,), (1,)), ((), ())), preferred_element_type=F32
    )
    gain = (jnp.repeat(band_gain, CELLS) / jnp.maximum(weight_sum, 1.0)).reshape(-1)
    bins = (my_patches[:, None] * TARGETS + jnp.arange(TARGETS, dtype=jnp.int32)).reshape(-1)
    near = lax.dynamic_index_in_dim(details, z, axis=0, keepdims=False)
    near_names = near[:, :3].astype(jnp.int32)
    near_patch, near_cell = near_names[:, 0], near_names[:, 1]
    near_key = near_patch * TARGETS + near_names[:, 2] * CELLS + near_cell
    near_gain = jnp.sum(jnp.where(near_key[..., None] == bins, gain, 0.0), axis=-1)
    near_scale = near_gain * near[:, 3]
    near_rank = ranks(near_patch)
    chosen = (near_patch[:, None, None, :] == my_patches[:, None, None]) & (
        near_rank[:, None, None, :] == jnp.arange(CAP, dtype=jnp.int32)[:, None]
    )
    scale = jnp.sum(jnp.where(chosen, near_scale[:, None, None, :], 0.0), axis=-1).reshape(-1)
    cell = jnp.sum(jnp.where(chosen, near_cell[:, None, None, :] + 1, 0), axis=-1).reshape(-1) - 1

    pieces = gather_slots(cell, scale, arrived).reshape(NZ, CR, STRIP, CC * B)
    taps = filter_taps.astype(BF16).astype(F32)
    return detect(taps, pieces)[None]


def solution(mesh):
    return jax.shard_map(
        local,
        mesh=mesh,
        in_specs=(
            P(None, ("sky", "band")),
            P(("sky", "band"), None),
            P(("sky", "band")),
            P(("sky", "band")),
            P(("sky", "band")),
            P(("sky", "band"), None),
            P(),
            P(),
            P(),
            P(),
        ),
        out_specs=P("sky", "band", None),
        check_vma=False,
    )
```

time: 340 us -> 159 us (0.47)
  the two profiles are of different devices: /device:TPU:56 before, /device:TPU:16 now
where the time goes in v2:
time: 159 us
  Pallas kernels  135 us (85%)
  local copies, waits for them, and re-layouts  15.2 us (10%)
  other arithmetic  7.09 us (4%)
    pallas_call x1, Pallas kernels, plane_exchange(): pl.pallas_call(plane_kernel, out_shape=(jax.ShapeDtypeStruct((PLANE, SLOT...  63.4 us
    pallas_call x1, Pallas kernels, detect(): pl.pallas_call(detect_kernel, out_shape=jax.ShapeDtypeStruct((B, CC * B),...  52.9 us
    pallas_call x1, Pallas kernels, match(): pl.pallas_call(match_kernel, out_shape=jax.ShapeDtypeStruct((PLANE * SLOT...  12.6 us
    unnamed x26, local copies, waits for them, and re-layouts  11.8 us
    pallas_call x1, Pallas kernels, gather_slots(): pl.pallas_call(gather_kernel, grid=(PLANE // per_step,), out_shape=jax.Sh...  6.42 us

profile of v2, /device:TPU:16, one launch (start us, length us, event | category | flops | bytes accessed | tf_op | source)
XLA Modules:
  0.0 158.5 jit_solution(17077243069698946482)
XLA Ops:
  0.0 0.7 convert_convert_fusion.taps_ref
  0.7 0.9 convert_reduce_fusion.1
  1.6 0.7 fusion.21.slot_ref
  2.3 0.8 copy.20.coef_ref
  3.1 1.5 copy-done.4
  4.6 0.7 copy-done.5
  5.3 0.7 copy-done.6
  5.9 12.6 %match.1 = bf16[512,32,128]{2,1,0:T(8,128)(2,1)S(1)} custom-call(s32[32]{0:T(128)S(1)} %fusion.21.slot_ref, f32[32,3]{1,0:T(8,128)S(1)} %copy.20.coef_ref, f32[3,41]{1,0:T(4,128)S(1)} %copy-done.5, f32[3,41]{1,0:T(4,128)S(1)} %copy-done.6, bf16[168,5376]{1,0:T(8,128)(2,1)S(1)} %copy-done.4), custom_call_target="tpu_custom_call" | custom-call | tf_op jit(solution)/shard_map/match/pallas_call | solution.py:120
  18.6 1.9 %copy-done = bf16[512,32,128]{2,1,0:T(8,128)(2,1)} copy-done((bf16[512,32,128]{2,1,0:T(8,128)(2,1)}, bf16[512,32,128]{2,1,0:T(8,128)(2,1)S(1)}, u32[]{:S(2)}) %copy-start) | copy-done | bytes 4194328
  20.6 2.2 %copy-done.1 = bf16[512,32,128]{2,1,0:T(8,128)(2,1)S(1)} copy-done((bf16[512,32,128]{2,1,0:T(8,128)(2,1)S(1)}, bf16[512,32,128]{2,1,0:T(8,128)(2,1)}, u32[]{:S(2)}) %copy-start.1) | copy-done | bytes 4194328
  22.8 63.4 %plane_exchange.1 = (bf16[32,16,32,128]{3,2,1,0:T(8,128)(2,1)S(1)}, f32[8,32,1,128]{3,2,1,0:T(1,128)S(1)}) custom-call(bf16[32,16,32,128]{3,2,1,0:T(8,128)(2,1)S(1)} %bitcast.37, f32[1,1,128]{2,1,0:T(1,128)S(1)} %reshape.146.info_ref), custom_call_target="tpu_custom_call" | custom-call | tf_op jit(solution)/shard_map/plane_exchange/pallas_call | solution.py:232
  86.2 1.9 %copy-done.2 = bf16[32,16,32,128]{3,2,1,0:T(8,128)(2,1)} copy-done((bf16[32,16,32,128]{3,2,1,0:T(8,128)(2,1)}, bf16[32,16,32,128]{3,2,1,0:T(8,128)(2,1)S(1)}, u32[]{:S(2)}) %copy-start.2) | copy-done | bytes 4194328
  88.2 0.5 broadcast.151
  88.7 1.0 reduce.15
  89.6 0.3 reshape.147
  90.0 0.8 convert_reduce_fusion
  90.8 0.1 broadcast_compare_fusion
  90.9 1.2 fusion.4
  92.2 0.1 copy.23
  92.4 0.1 sub.19.cell_ref
  92.5 1.0 fusion.8
  93.6 0.4 slice_reduce_fusion
  94.0 0.1 reshape_squeeze.3
  94.4 0.7 fusion.3
  95.3 0.5 select_reduce_fusion
  95.7 0.2 fusion.5
  95.9 0.3 copy.24
  96.2 0.1 reshape.149.scale_ref
  96.3 2.2 %copy-done.3 = bf16[32,16,32,128]{3,2,1,0:T(8,128)(2,1)S(1)} copy-done((bf16[32,16,32,128]{3,2,1,0:T(8,128)(2,1)S(1)}, bf16[32,16,32,128]{3,2,1,0:T(8,128)(2,1)}, u32[]{:S(2)}) %copy-start.3) | copy-done | bytes 4194328
  98.5 6.4 %gather_slots.1 = bf16[32,32,512]{2,1,0:T(8,128)(2,1)S(1)} custom-call(s32[512]{0:T(512)S(1)} %sub.19.cell_ref, f32[512]{0:T(512)S(1)} %reshape.149.scale_ref, bf16[32,16,32,128]{3,2,1,0:T(8,128)(2,1)S(1)} %copy-done.3), custom_call_target="tpu_custom_call" | custom-call | tf_op jit(solution)/shard_map/gather_slots/pallas_call | solution.py:294
  104.9 52.9 %detect.1 = f32[128,512]{1,0:T(8,128)S(1)} custom-call(f32[41]{0:T(128)S(1)} %convert_convert_fusion.taps_ref, bf16[8,4,32,512]{3,2,1,0:T(8,128)(2,1)S(1)} %bitcast.38), custom_call_target="tpu_custom_call" | custom-call | tf_op jit(solution)/shard_map/detect/pallas_call | solution.py:450
  157.8 0.7 copy.29
  (40 shorter events, 0.8 us)
Async XLA Ops:
  0.0 20.5 %copy-start.11 = (s32[32,1]{0,1:T(1,128)S(1)}, s32[32,1]{0,1:T(1,128)}, u32[]{:S(2)}) copy-start(s32[32,1]{0,1:T(1,128)} %param.11) | copy-start | bytes 388
  0.0 20.5 %copy-start.10 = (bf16[32]{0:T(256)(128)(2,1)S(1)}, bf16[32]{0:T(256)(128)(2,1)}, u32[]{:S(2)}) copy-start(bf16[32]{0:T(256)(128)(2,1)} %param.14) | copy-start | bytes 196
  0.0 20.5 %copy-start.8 = (s32[32]{0:T(128)S(1)}, s32[32]{0:T(128)}, u32[]{:S(2)}) copy-start(s32[32]{0:T(128)} %param.13) | copy-start | bytes 388
  0.0 20.5 %copy-start.9 = (s32[32]{0:T(128)S(1)}, s32[32]{0:T(128)}, u32[]{:S(2)}) copy-start(s32[32]{0:T(128)} %param.12) | copy-start | bytes 388
  3.1 1.5 copy-start.4
  4.6 0.7 copy-start.5
  5.2 0.7 copy-start.6
  18.6 1.9 %copy-start = (bf16[512,32,128]{2,1,0:T(8,128)(2,1)}, bf16[512,32,128]{2,1,0:T(8,128)(2,1)S(1)}, u32[]{:S(2)}) copy-start(bf16[512,32,128]{2,1,0:T(8,128)(2,1)S(1)} %match.1) | copy-start | bytes 12582916
  20.6 2.2 %copy-start.1 = (bf16[512,32,128]{2,1,0:T(8,128)(2,1)S(1)}, bf16[512,32,128]{2,1,0:T(8,128)(2,1)}, u32[]{:S(2)}) copy-start(bf16[512,32,128]{2,1,0:T(8,128)(2,1)} %copy-done) | copy-start | bytes 12582916
  22.8 71.4 %copy-start.7 = (f32[6]{0:T(128)S(1)}, f32[6]{0:T(128)}, u32[]{:S(2)}) copy-start(f32[6]{0:T(128)} %param.18) | copy-start | bytes 76
  86.2 1.9 %copy-start.2 = (bf16[32,16,32,128]{3,2,1,0:T(8,128)(2,1)}, bf16[32,16,32,128]{3,2,1,0:T(8,128)(2,1)S(1)}, u32[]{:S(2)}) copy-start(bf16[32,16,32,128]{3,2,1,0:T(8,128)(2,1)S(1)} %get-tuple-element.8.in_ref) | copy-start | bytes 12582916
  96.3 2.2 %copy-start.3 = (bf16[32,16,32,128]{3,2,1,0:T(8,128)(2,1)S(1)}, bf16[32,16,32,128]{3,2,1,0:T(8,128)(2,1)}, u32[]{:S(2)}) copy-start(bf16[32,16,32,128]{3,2,1,0:T(8,128)(2,1)} %copy-done.2) | copy-start | bytes 12582916

commit v3 on v2

--- a/solution.py
+++ b/solution.py
@@ -25,6 +25,14 @@
 STRIP = B // NY
 ROWS = B + 2 * STRIP
 MESH = pl.DeviceIdType.MESH
+HALFWAY = ((2, 2), (2, 0), (0, 2), (2, 1), (1, 2), (2, 3), (3, 2))
+RELAYED = tuple((dx, 1, dy) for dx, dy in HALFWAY)
+DIRECT = tuple((dx, 0, dy) for dx, dy in HALFWAY) + tuple(
+    (dx, dc, dy)
+    for dx, dy in ((1, 3), (3, 1), (1, 1), (3, 3), (1, 0), (3, 0), (0, 1), (0, 3), (0, 0))
+    for dc in range(NC)
+    if (dx, dc, dy) != (0, 0, 0)
+)
 F32 = jnp.float32
 BF16 = jnp.bfloat16
 
@@ -132,10 +140,9 @@
     )(slot, coef, row_basis, col_basis, raw)
 
 
-def plane_device(index, z):
-    return device(
-        lax.div(index, NC * NY), z, lax.rem(lax.div(index, NY), NC), lax.rem(index, NY)
-    )
+def offset_id(offset):
+    dx, dc, dy = offset
+    return (dx * NC + dc) * NY + dy
 
 
 def plane_kernel(
@@ -144,8 +151,11 @@
     in_ref,
     every_ref,
     own,
+    passing,
     send_sem,
     recv_sem,
+    pass_send,
+    pass_recv,
     info_send,
     info_recv,
     z_send,
@@ -155,14 +165,20 @@
 ):
     x, z, core, y = coordinates()
     me = (x * NC + core) * NY + y
+
+    def moved(dx, dc, dy):
+        return lax.rem(x + dx, NX), lax.rem(core + dc, NC), lax.rem(y + dy, NY)
+
+    def index(place):
+        return (place[0] * NC + place[1]) * NY + place[2]
+
+    def at(place):
+        return device(place[0], z, place[1], place[2])
+
+    everyone = RELAYED + DIRECT
     barrier = pltpu.get_barrier_semaphore()
-    for step in range(1, PLANE):
-        pl.semaphore_signal(
-            barrier,
-            inc=1,
-            device_id=plane_device(lax.rem(me + step, PLANE), z),
-            device_id_type=MESH,
-        )
+    for offset in everyone:
+        pl.semaphore_signal(barrier, inc=1, device_id=at(moved(*offset)), device_id_type=MESH)
     for step in range(1, NZ):
         pl.semaphore_signal(
             barrier,
@@ -176,26 +192,38 @@
     keep.start()
     pl.semaphore_wait(barrier, PLANE - 1 + NZ - 1)
     infos = []
-    for step in range(1, PLANE):
+    for offset in everyone:
         copy = pltpu.make_async_remote_copy(
             src_ref=info_ref.at[0],
             dst_ref=every_ref.at[z, me],
-            send_sem=info_send.at[step],
-            recv_sem=info_recv.at[step],
-            device_id=plane_device(lax.rem(me + step, PLANE), z),
+            send_sem=info_send.at[offset_id(offset)],
+            recv_sem=info_recv.at[offset_id(offset)],
+            device_id=at(moved(*offset)),
             device_id_type=MESH,
         )
         copy.start()
         infos.append(copy)
+    firsts = []
+    for k, (dx, dc, dy) in enumerate(RELAYED):
+        back_x, back_y = (NX - 1) * (dx == 2), (NY - 1) * (dy == 2)
+        copy = pltpu.make_async_remote_copy(
+            src_ref=out_ref.at[index(moved(dx, dc, dy))],
+            dst_ref=passing.at[k],
+            send_sem=pass_send.at[k],
+            recv_sem=pass_recv.at[k],
+            device_id=at(moved(back_x, 0, back_y)),
+            device_id_type=MESH,
+        )
+        copy.start()
+        firsts.append(copy)
     copies = []
-    for step in range(1, PLANE):
-        peer = lax.rem(me + step, PLANE)
+    for offset in DIRECT:
         copy = pltpu.make_async_remote_copy(
-            src_ref=out_ref.at[peer],
+            src_ref=out_ref.at[index(moved(*offset))],
             dst_ref=in_ref.at[me],
-            send_sem=send_sem.at[step],
-            recv_sem=recv_sem.at[step],
-            device_id=plane_device(peer, z),
+            send_sem=send_sem.at[offset_id(offset)],
+            recv_sem=recv_sem.at[offset_id(offset)],
+            device_id=at(moved(*offset)),
             device_id_type=MESH,
         )
         copy.start()
@@ -218,9 +246,25 @@
         )
         copy.start()
         planes.append(copy)
+    for k, offset in enumerate(RELAYED):
+        dx, dc, dy = offset
+        ahead_x, ahead_y = dx == 2, dy == 2
+        firsts[k].wait_recv()
+        copy = pltpu.make_async_remote_copy(
+            src_ref=passing.at[k],
+            dst_ref=in_ref.at[index(moved(int(ahead_x), 0, int(ahead_y)))],
+            send_sem=send_sem.at[offset_id(offset)],
+            recv_sem=recv_sem.at[offset_id(offset)],
+            device_id=at(moved((dx + ahead_x) % NX, dc, (dy + ahead_y) % NY)),
+            device_id_type=MESH,
+        )
+        copy.start()
+        copies.append(copy)
     put.wait()
     for copy in planes:
         copy.wait()
+    for copy in firsts:
+        copy.wait_send()
     for copy in copies:
         copy.wait()
 
@@ -236,11 +280,14 @@
             jax.ShapeDtypeStruct((NZ, PLANE, 1, B), F32),
         ),
         in_specs=[hbm, vmem],
-        out_specs=(hbm, vmem),
+        out_specs=(pl.BlockSpec(memory_space=pltpu.HBM), vmem),
         scratch_shapes=[
             pltpu.VMEM((SLOTS, STRIP, B), BF16),
+            pltpu.VMEM((len(RELAYED), SLOTS, STRIP, B), BF16),
             dma((PLANE,)),
             dma((PLANE,)),
+            dma((len(RELAYED),)),
+            dma((len(RELAYED),)),
             dma((PLANE,)),
             dma((PLANE,)),
             dma((NZ,)),
@@ -308,6 +355,7 @@
     piece_ref,
     out_ref,
     held,
+    passing,
     strips,
     window,
     rowf,
@@ -315,6 +363,8 @@
     padded,
     z_send,
     z_recv,
+    far_send,
+    far_recv,
     y_send,
     y_recv,
     edge_send,
@@ -341,7 +391,28 @@
     keep.start()
     pl.semaphore_wait(barrier, NZ - 1 + NY - 1)
     pieces = []
-    for step in (4, 3, 5, 2, 6, 1, 7):
+    half = CR // 2
+    far = lax.rem(z + NZ // 2, NZ)
+    first = pltpu.make_async_remote_copy(
+        src_ref=piece_ref.at[far, pl.ds(half, half)],
+        dst_ref=passing,
+        send_sem=far_send.at[0],
+        recv_sem=far_recv.at[0],
+        device_id=device(x, lax.rem(z + NZ - 1, NZ), core, y),
+        device_id_type=MESH,
+    )
+    first.start()
+    direct = pltpu.make_async_remote_copy(
+        src_ref=piece_ref.at[far, pl.ds(0, half)],
+        dst_ref=held.at[z, pl.ds(0, half)],
+        send_sem=far_send.at[1],
+        recv_sem=far_recv.at[1],
+        device_id=device(x, far, core, y),
+        device_id_type=MESH,
+    )
+    direct.start()
+    pieces.append(direct)
+    for step in (3, 5, 2, 6, 1, 7):
         peer = lax.rem(z + step, NZ)
         copy = pltpu.make_async_remote_copy(
             src_ref=piece_ref.at[peer],
@@ -368,7 +439,19 @@
     padded[:, :B] = jnp.zeros((B, B), BF16)
     padded[:, B + CC * B :] = jnp.zeros((B, B), BF16)
 
+    first.wait_recv()
+    second = pltpu.make_async_remote_copy(
+        src_ref=passing,
+        dst_ref=held.at[lax.rem(z + 1, NZ), pl.ds(half, half)],
+        send_sem=far_send.at[2],
+        recv_sem=far_recv.at[2],
+        device_id=device(x, lax.rem(z + 1 + NZ // 2, NZ), core, y),
+        device_id_type=MESH,
+    )
+    second.start()
+    pieces.append(second)
     keep.wait()
+    first.wait_send()
     for copy in pieces:
         copy.wait()
     for r in range(CR):
@@ -454,6 +537,7 @@
         out_specs=pl.BlockSpec(memory_space=pltpu.VMEM),
         scratch_shapes=[
             pltpu.VMEM((NZ, CR, STRIP, CC * B), BF16),
+            pltpu.VMEM((CR // 2, STRIP, CC * B), BF16),
             pltpu.VMEM((CR, STRIP, CC * B), BF16),
             pltpu.VMEM((NY + 2, STRIP, CC * B), BF16),
             pltpu.VMEM((B, 256), BF16),
@@ -461,6 +545,8 @@
             pltpu.VMEM((B, (CC + 2) * B), BF16),
             dma((NZ,)),
             dma((NZ,)),
+            dma((3,)),
+            dma((3,)),
             dma((NY,)),
             dma((NY,)),
             dma((NY,)),
@@ -501,9 +587,10 @@
     patch_z = patch // NC % NZ
     patch_x = patch // (NC * NZ)
     slot = (patch_x * NC + patch_core) * (NY * SLOTS) + patch_z * CAP + ranks(patch)
+    info, slot = lax.optimization_barrier((own_details.reshape(1, 1, 4 * BLK), slot))
     outgoing = match(slot, basis_coef.astype(F32), row_basis, col_basis, raw_blocks)
     arrived, details = plane_exchange(
-        outgoing.reshape(PLANE, SLOTS, STRIP, B), own_details.reshape(1, 1, 4 * BLK)
+        outgoing.reshape(PLANE, SLOTS, STRIP, B), info
     )
     details = details.reshape(NZ, PLANE, 4, BLK)
 
@@ -532,8 +619,7 @@
     cell = jnp.sum(jnp.where(chosen, near_cell[:, None, None, :] + 1, 0), axis=-1).reshape(-1) - 1
 
     pieces = gather_slots(cell, scale, arrived).reshape(NZ, CR, STRIP, CC * B)
-    taps = filter_taps.astype(BF16).astype(F32)
-    return detect(taps, pieces)[None]
+    return detect(filter_taps, pieces)[None]
 
 
 def solution(mesh):

time: 159 us -> 151 us (0.950)
  Pallas kernels: 135 us -> 129 us
  local copies, waits for them, and re-layouts: 15.2 us -> 11.1 us
    pallas_call x1, Pallas kernels: 52.9 us -> 36.8 us  [detect(): pl.pallas_call(detect_kernel, out_shape=jax.ShapeDtypeStruct((B, CC * B),...]
    pallas_call x1, Pallas kernels: 63.4 us -> 72.8 us  [plane_exchange(): pl.pallas_call(plane_kernel, out_shape=(jax.ShapeDtypeStruct((PLANE, SLOT...]
    unnamed x26 -> x16, local copies, waits for them, and re-layouts: 11.8 us -> 7.68 us
where the time goes in v3:
time: 151 us; the launch traced here: 149 us
  Pallas kernels  129 us (85%)
  local copies, waits for them, and re-layouts  11.1 us (7%)
  other arithmetic  8.37 us (6%)
    pallas_call x1, Pallas kernels, plane_exchange(): pl.pallas_call(plane_kernel, out_shape=(jax.ShapeDtypeStruct((PLANE, SLOT...  72.8 us
    pallas_call x1, Pallas kernels, detect(): pl.pallas_call(detect_kernel, out_shape=jax.ShapeDtypeStruct((B, CC * B),...  36.8 us
    pallas_call x1, Pallas kernels, match(): pl.pallas_call(match_kernel, out_shape=jax.ShapeDtypeStruct((PLANE * SLOT...  12.6 us
    unnamed x16, local copies, waits for them, and re-layouts  7.68 us
    pallas_call x1, Pallas kernels, gather_slots(): pl.pallas_call(gather_kernel, grid=(PLANE // per_step,), out_shape=jax.Sh...  6.72 us

profile of v3, /device:TPU:16, one launch (start us, length us, event | category | flops | bytes accessed | tf_op | source)
XLA Modules:
  0.0 149.2 jit_solution(4929494804435535585)
XLA Ops:
  0.0 0.7 bitcast_convert_fusion
  0.7 0.7 convert_bitcast_fusion
  1.3 0.7 convert_bitcast_fusion.2
  2.1 0.9 convert_reduce_fusion.1
  3.0 0.7 fusion.21.slot_ref
  3.7 0.8 copy.20.coef_ref
  4.4 1.5 copy-done.2
  5.9 0.7 copy-done.3
  6.6 0.7 copy-done.4
  7.3 12.6 %match.1 = bf16[512,32,128]{2,1,0:T(8,128)(2,1)S(1)} custom-call(s32[32]{0:T(128)S(1)} %fusion.21.slot_ref, f32[32,3]{1,0:T(8,128)S(1)} %copy.20.coef_ref, f32[3,41]{1,0:T(4,128)S(1)} %copy-done.3, f32[3,41]{1,0:T(4,128)S(1)} %copy-done.4, bf16[168,5376]{1,0:T(8,128)(2,1)S(1)} %copy-done.2), custom_call_target="tpu_custom_call" | custom-call | tf_op jit(solution)/shard_map/match/pallas_call | solution.py:128
  20.0 72.8 %plane_exchange.1 = (bf16[32,16,32,128]{3,2,1,0:T(8,128)(2,1)S(1)}, f32[8,32,1,128]{3,2,1,0:T(1,128)S(1)}) custom-call(bf16[32,16,32,128]{3,2,1,0:T(8,128)(2,1)S(1)} %bitcast.37, f32[1,1,128]{2,1,0:T(1,128)S(1)} %reshape.145.info_ref), custom_call_target="tpu_custom_call" | custom-call | tf_op jit(solution)/shard_map/plane_exchange/pallas_call | solution.py:276
  92.7 1.9 %copy-done = bf16[32,16,32,128]{3,2,1,0:T(8,128)(2,1)} copy-done((bf16[32,16,32,128]{3,2,1,0:T(8,128)(2,1)}, bf16[32,16,32,128]{3,2,1,0:T(8,128)(2,1)S(1)}, u32[]{:S(2)}) %copy-start) | copy-done | bytes 4194328
  94.6 0.5 broadcast.151
  95.2 1.0 reduce.15
  96.1 0.3 reshape.147
  96.5 0.8 convert_reduce_fusion
  97.3 0.1 broadcast_compare_fusion
  97.4 1.2 fusion.4
  98.7 0.1 copy.23
  98.9 0.1 sub.19.cell_ref
  99.0 1.0 fusion.8
  100.1 0.4 slice_reduce_fusion
  100.5 0.1 reshape_squeeze.3
  100.9 0.7 fusion.3
  101.8 0.5 select_reduce_fusion
  102.2 0.2 fusion.5
  102.4 0.3 copy.24
  102.7 0.1 reshape.149.scale_ref
  102.8 2.2 %copy-done.1 = bf16[32,16,32,128]{3,2,1,0:T(8,128)(2,1)S(1)} copy-done((bf16[32,16,32,128]{3,2,1,0:T(8,128)(2,1)S(1)}, bf16[32,16,32,128]{3,2,1,0:T(8,128)(2,1)}, u32[]{:S(2)}) %copy-start.1) | copy-done | bytes 4194328
  105.0 6.7 %gather_slots.1 = bf16[32,32,512]{2,1,0:T(8,128)(2,1)S(1)} custom-call(s32[512]{0:T(512)S(1)} %sub.19.cell_ref, f32[512]{0:T(512)S(1)} %reshape.149.scale_ref, bf16[32,16,32,128]{3,2,1,0:T(8,128)(2,1)S(1)} %copy-done.1), custom_call_target="tpu_custom_call" | custom-call | tf_op jit(solution)/shard_map/gather_slots/pallas_call | solution.py:341
  111.8 36.8 %detect.1 = f32[128,512]{1,0:T(8,128)S(1)} custom-call(f32[41]{0:T(128)S(1)} %copy-done.5, bf16[8,4,32,512]{3,2,1,0:T(8,128)(2,1)S(1)} %bitcast.38), custom_call_target="tpu_custom_call" | custom-call | tf_op jit(solution)/shard_map/detect/pallas_call | solution.py:533
  148.5 0.7 copy.29
  (29 shorter events, 0.8 us)
Async XLA Ops:
  4.4 1.5 copy-start.2
  5.9 0.7 copy-start.3
  6.6 0.7 copy-start.4
  19.9 80.8 %copy-start.6 = (f32[6]{0:T(128)S(1)}, f32[6]{0:T(128)}, u32[]{:S(2)}) copy-start(f32[6]{0:T(128)} %param.18) | copy-start | bytes 76
  92.7 1.9 %copy-start = (bf16[32,16,32,128]{3,2,1,0:T(8,128)(2,1)}, bf16[32,16,32,128]{3,2,1,0:T(8,128)(2,1)S(1)}, u32[]{:S(2)}) copy-start(bf16[32,16,32,128]{3,2,1,0:T(8,128)(2,1)S(1)} %get-tuple-element.12.in_ref) | copy-start | bytes 12582916
  100.9 10.9 %copy-start.5 = (f32[41]{0:T(128)S(1)}, f32[41]{0:T(128)}, u32[]{:S(2)}) copy-start(f32[41]{0:T(128)} %taps_ref.1) | copy-start | bytes 496
  102.8 2.2 %copy-start.1 = (bf16[32,16,32,128]{3,2,1,0:T(8,128)(2,1)S(1)}, bf16[32,16,32,128]{3,2,1,0:T(8,128)(2,1)}, u32[]{:S(2)}) copy-start(bf16[32,16,32,128]{3,2,1,0:T(8,128)(2,1)} %copy-done) | copy-start | bytes 12582916

commit v4 on v3

--- a/solution.py
+++ b/solution.py
@@ -27,11 +27,17 @@
 MESH = pl.DeviceIdType.MESH
 HALFWAY = ((2, 2), (2, 0), (0, 2), (2, 1), (1, 2), (2, 3), (3, 2))
 RELAYED = tuple((dx, 1, dy) for dx, dy in HALFWAY)
-DIRECT = tuple((dx, 0, dy) for dx, dy in HALFWAY) + tuple(
+EARLY = tuple(
     (dx, dc, dy)
-    for dx, dy in ((1, 3), (3, 1), (1, 1), (3, 3), (1, 0), (3, 0), (0, 1), (0, 3), (0, 0))
+    for dx, dy in ((2, 2), (2, 0), (0, 2), (2, 1), (1, 2), (1, 1), (1, 0), (0, 1), (0, 0))
     for dc in range(NC)
-    if (dx, dc, dy) != (0, 0, 0)
+    if (dx, dc, dy) != (0, 0, 0) and (dx, dc, dy) not in RELAYED
+)
+LATE = tuple(
+    (dx, dc, dy)
+    for dx, dy in ((2, 3), (3, 2), (3, 3), (1, 3), (3, 1), (3, 0), (0, 3))
+    for dc in range(NC)
+    if (dx, dc, dy) not in RELAYED
 )
 F32 = jnp.float32
 BF16 = jnp.bfloat16
@@ -175,7 +181,7 @@
     def at(place):
         return device(place[0], z, place[1], place[2])
 
-    everyone = RELAYED + DIRECT
+    everyone = RELAYED + EARLY + LATE
     barrier = pltpu.get_barrier_semaphore()
     for offset in everyone:
         pl.semaphore_signal(barrier, inc=1, device_id=at(moved(*offset)), device_id_type=MESH)
@@ -217,7 +223,8 @@
         copy.start()
         firsts.append(copy)
     copies = []
-    for offset in DIRECT:
+
+    def send(offset):
         copy = pltpu.make_async_remote_copy(
             src_ref=out_ref.at[index(moved(*offset))],
             dst_ref=in_ref.at[me],
@@ -228,9 +235,28 @@
         )
         copy.start()
         copies.append(copy)
+
+    for offset in EARLY:
+        send(offset)
     take.wait()
     put = pltpu.make_async_copy(own, in_ref.at[me], own_sem)
     put.start()
+    for k, offset in enumerate(RELAYED):
+        dx, dc, dy = offset
+        ahead_x, ahead_y = dx == 2, dy == 2
+        firsts[k].wait_recv()
+        copy = pltpu.make_async_remote_copy(
+            src_ref=passing.at[k],
+            dst_ref=in_ref.at[index(moved(int(ahead_x), 0, int(ahead_y)))],
+            send_sem=send_sem.at[offset_id(offset)],
+            recv_sem=recv_sem.at[offset_id(offset)],
+            device_id=at(moved((dx + ahead_x) % NX, dc, (dy + ahead_y) % NY)),
+            device_id_type=MESH,
+        )
+        copy.start()
+        copies.append(copy)
+    for offset in LATE:
+        send(offset)
     keep.wait()
     for copy in infos:
         copy.wait()
@@ -246,20 +272,6 @@
         )
         copy.start()
         planes.append(copy)
-    for k, offset in enumerate(RELAYED):
-        dx, dc, dy = offset
-        ahead_x, ahead_y = dx == 2, dy == 2
-        firsts[k].wait_recv()
-        copy = pltpu.make_async_remote_copy(
-            src_ref=passing.at[k],
-            dst_ref=in_ref.at[index(moved(int(ahead_x), 0, int(ahead_y)))],
-            send_sem=send_sem.at[offset_id(offset)],
-            recv_sem=recv_sem.at[offset_id(offset)],
-            device_id=at(moved((dx + ahead_x) % NX, dc, (dy + ahead_y) % NY)),
-            device_id_type=MESH,
-        )
-        copy.start()
-        copies.append(copy)
     put.wait()
     for copy in planes:
         copy.wait()
@@ -345,7 +357,7 @@
         in_specs=[smem, smem, pl.BlockSpec((per_step, SLOTS, STRIP, B), lambda i: (i, 0, 0, 0))],
         out_specs=pl.BlockSpec(shape, lambda i: (0, 0, 0)),
         scratch_shapes=[pltpu.VMEM(shape, F32)],
-        compiler_params=pltpu.CompilerParams(vmem_limit_bytes=16 * 1024 * 1024),
+        compiler_params=pltpu.CompilerParams(vmem_limit_bytes=60 * 1024 * 1024),
         name="gather_slots",
     )(cell, scale, arrived)
 
@@ -412,7 +424,8 @@
     )
     direct.start()
     pieces.append(direct)
-    for step in (3, 5, 2, 6, 1, 7):
+
+    def send(step):
         peer = lax.rem(z + step, NZ)
         copy = pltpu.make_async_remote_copy(
             src_ref=piece_ref.at[peer],
@@ -424,6 +437,22 @@
         )
         copy.start()
         pieces.append(copy)
+
+    for step in (3, 2, 1, 7):
+        send(step)
+    first.wait_recv()
+    second = pltpu.make_async_remote_copy(
+        src_ref=passing,
+        dst_ref=held.at[lax.rem(z + 1, NZ), pl.ds(half, half)],
+        send_sem=far_send.at[2],
+        recv_sem=far_recv.at[2],
+        device_id=device(x, lax.rem(z + 1 + NZ // 2, NZ), core, y),
+        device_id_type=MESH,
+    )
+    second.start()
+    pieces.append(second)
+    for step in (5, 6):
+        send(step)
 
     def tap(k, t):
         return taps_ref[t]
@@ -439,17 +468,6 @@
     padded[:, :B] = jnp.zeros((B, B), BF16)
     padded[:, B + CC * B :] = jnp.zeros((B, B), BF16)
 
-    first.wait_recv()
-    second = pltpu.make_async_remote_copy(
-        src_ref=passing,
-        dst_ref=held.at[lax.rem(z + 1, NZ), pl.ds(half, half)],
-        send_sem=far_send.at[2],
-        recv_sem=far_recv.at[2],
-        device_id=device(x, lax.rem(z + 1 + NZ // 2, NZ), core, y),
-        device_id_type=MESH,
-    )
-    second.start()
-    pieces.append(second)
     keep.wait()
     first.wait_send()
     for copy in pieces:
@@ -580,13 +598,13 @@
 ):
     x, z, core, y = coordinates()
     patch = patch_of_block[:, 0]
-    own_details = jnp.stack(
-        [v.astype(F32) for v in (patch, cell_of_block, band_of_block, block_weight)]
-    )
+    rank = ranks(patch)
+    target = band_of_block * CELLS + cell_of_block
+    own_details = jnp.stack([v.astype(F32) for v in (patch, target, rank, block_weight)])
     patch_core = patch % NC
     patch_z = patch // NC % NZ
     patch_x = patch // (NC * NZ)
-    slot = (patch_x * NC + patch_core) * (NY * SLOTS) + patch_z * CAP + ranks(patch)
+    slot = (patch_x * NC + patch_core) * (NY * SLOTS) + patch_z * CAP + rank
     info, slot = lax.optimization_barrier((own_details.reshape(1, 1, 4 * BLK), slot))
     outgoing = match(slot, basis_coef.astype(F32), row_basis, col_basis, raw_blocks)
     arrived, details = plane_exchange(
@@ -596,7 +614,7 @@
 
     my_patches = (x * NZ + jnp.arange(NZ, dtype=jnp.int32)) * NC + core
     every_patch = details[:, :, 0].astype(jnp.int32).reshape(-1)
-    every_target = (details[:, :, 2] * CELLS + details[:, :, 1]).astype(jnp.int32).reshape(-1)
+    every_target = details[:, :, 1].astype(jnp.int32).reshape(-1)
     every_weight = details[:, :, 3].reshape(-1)
     share = jnp.where(every_patch == my_patches[:, None], every_weight, 0.0).astype(BF16)
     hits = (every_target == jnp.arange(TARGETS, dtype=jnp.int32)[:, None]).astype(BF16)
@@ -607,11 +625,11 @@
     bins = (my_patches[:, None] * TARGETS + jnp.arange(TARGETS, dtype=jnp.int32)).reshape(-1)
     near = lax.dynamic_index_in_dim(details, z, axis=0, keepdims=False)
     near_names = near[:, :3].astype(jnp.int32)
-    near_patch, near_cell = near_names[:, 0], near_names[:, 1]
-    near_key = near_patch * TARGETS + near_names[:, 2] * CELLS + near_cell
+    near_patch, near_target, near_rank = near_names[:, 0], near_names[:, 1], near_names[:, 2]
+    near_cell = near_target % CELLS
+    near_key = near_patch * TARGETS + near_target
     near_gain = jnp.sum(jnp.where(near_key[..., None] == bins, gain, 0.0), axis=-1)
     near_scale = near_gain * near[:, 3]
-    near_rank = ranks(near_patch)
     chosen = (near_patch[:, None, None, :] == my_patches[:, None, None]) & (
         near_rank[:, None, None, :] == jnp.arange(CAP, dtype=jnp.int32)[:, None]
     )

time: 151 us -> 157 us (1.040)
  Pallas kernels: 129 us -> 135 us
    pallas_call x1, Pallas kernels: 36.8 us -> 40.7 us  [detect(): pl.pallas_call(detect_kernel, out_shape=jax.ShapeDtypeStruct((B, CC * B),...]
    pallas_call x1, Pallas kernels: 6.72 us -> 9.24 us  [gather_slots(): pl.pallas_call(gather_kernel, grid=(PLANE // per_step,), out_shape=jax.Sh...]
where the time goes in v4:
time: 157 us; the launch traced here: 154 us
  Pallas kernels  135 us (86%)
  local copies, waits for them, and re-layouts  11.3 us (7%)
  other arithmetic  7.42 us (5%)
    pallas_call x1, Pallas kernels, plane_exchange(): pl.pallas_call(plane_kernel, out_shape=(jax.ShapeDtypeStruct((PLANE, SLOT...  72.1 us
    pallas_call x1, Pallas kernels, detect(): pl.pallas_call(detect_kernel, out_shape=jax.ShapeDtypeStruct((B, CC * B),...  40.7 us
    pallas_call x1, Pallas kernels, match(): pl.pallas_call(match_kernel, out_shape=jax.ShapeDtypeStruct((PLANE * SLOT...  12.6 us
    pallas_call x1, Pallas kernels, gather_slots(): pl.pallas_call(gather_kernel, grid=(PLANE // per_step,), out_shape=jax.Sh...  9.24 us
    unnamed x16, local copies, waits for them, and re-layouts  6.72 us

profile of v4, /device:TPU:16, one launch (start us, length us, event | category | flops | bytes accessed | tf_op | source)
XLA Modules:
  0.0 154.2 jit_solution(8159341448275174840)
XLA Ops:
  0.0 0.7 bitcast_convert_fusion
  0.7 0.9 convert_reduce_fusion
  1.6 0.7 fusion.19
  2.2 0.7 convert_bitcast_fusion.1
  2.9 0.7 convert_bitcast_fusion.2
  3.7 0.8 copy.21.coef_ref
  4.5 1.5 copy-done.2
  5.9 0.7 copy-done.3
  6.6 0.7 copy-done.4
  7.3 12.6 %match.1 = bf16[512,32,128]{2,1,0:T(8,128)(2,1)S(1)} custom-call(s32[32]{0:T(128)S(1)} %get-tuple-element.9.slot_ref, f32[32,3]{1,0:T(8,128)S(1)} %copy.21.coef_ref, f32[3,41]{1,0:T(4,128)S(1)} %copy-done.3, f32[3,41]{1,0:T(4,128)S(1)} %copy-done.4, bf16[168,5376]{1,0:T(8,128)(2,1)S(1)} %copy-done.2), custom_call_target="tpu_custom_call" | custom-call | tf_op jit(solution)/shard_map/match/pallas_call | solution.py:134
  19.9 72.1 %plane_exchange.1 = (bf16[32,16,32,128]{3,2,1,0:T(8,128)(2,1)S(1)}, f32[8,32,1,128]{3,2,1,0:T(1,128)S(1)}) custom-call(bf16[32,16,32,128]{3,2,1,0:T(8,128)(2,1)S(1)} %bitcast.33, f32[1,1,128]{2,1,0:T(1,128)S(1)} %reshape.139.info_ref), custom_call_target="tpu_custom_call" | custom-call | tf_op jit(solution)/shard_map/plane_exchange/pallas_call | solution.py:288
  92.1 1.9 %copy-done = bf16[32,16,32,128]{3,2,1,0:T(8,128)(2,1)} copy-done((bf16[32,16,32,128]{3,2,1,0:T(8,128)(2,1)}, bf16[32,16,32,128]{3,2,1,0:T(8,128)(2,1)S(1)}, u32[]{:S(2)}) %copy-start) | copy-done | bytes 4194328
  94.0 0.5 broadcast.160
  94.5 1.0 reduce.15
  95.5 0.3 reshape.141
  95.9 0.1 broadcast_compare_fusion
  96.0 1.2 fusion.4
  97.3 0.1 copy.24
  97.4 0.7 sub.19.cell_ref
  98.1 0.8 fusion.7
  99.1 0.4 slice_reduce_fusion
  99.5 0.1 reshape_squeeze.3
  99.6 0.1 convert_element_type.72
  99.8 0.7 fusion.3
  100.7 0.5 select_reduce_fusion
  101.2 0.2 fusion.5
  101.4 0.3 copy.25
  101.6 0.7 reshape.143.scale_ref
  102.4 9.2 %gather_slots.1 = bf16[32,32,512]{2,1,0:T(8,128)(2,1)} custom-call(s32[512]{0:T(512)} %sub.19.cell_ref, f32[512]{0:T(512)} %reshape.143.scale_ref, bf16[32,16,32,128]{3,2,1,0:T(8,128)(2,1)} %copy-done), custom_call_target="tpu_custom_call" | custom-call | tf_op jit(solution)/shard_map/gather_slots/pallas_call | solution.py:353
  111.6 1.2 copy-done.1
  112.8 40.7 %detect.1 = f32[128,512]{1,0:T(8,128)S(1)} custom-call(f32[41]{0:T(128)S(1)} %copy-done.5, bf16[8,4,32,512]{3,2,1,0:T(8,128)(2,1)S(1)} %bitcast.34), custom_call_target="tpu_custom_call" | custom-call | tf_op jit(solution)/shard_map/detect/pallas_call | solution.py:551
  153.5 0.7 copy.30
  (27 shorter events, 0.7 us)
Async XLA Ops:
  4.4 1.5 copy-start.2
  5.9 0.7 copy-start.3
  6.6 0.7 copy-start.4
  19.9 79.7 %copy-start.6 = (f32[6]{0:T(128)S(1)}, f32[6]{0:T(128)}, u32[]{:S(2)}) copy-start(f32[6]{0:T(128)} %param.18) | copy-start | bytes 76
  92.1 1.9 %copy-start = (bf16[32,16,32,128]{3,2,1,0:T(8,128)(2,1)}, bf16[32,16,32,128]{3,2,1,0:T(8,128)(2,1)S(1)}, u32[]{:S(2)}) copy-start(bf16[32,16,32,128]{3,2,1,0:T(8,128)(2,1)S(1)} %get-tuple-element.12.in_ref) | copy-start | bytes 12582916
  99.8 11.8 %copy-start.5 = (f32[41]{0:T(128)S(1)}, f32[41]{0:T(128)}, u32[]{:S(2)}) copy-start(f32[41]{0:T(128)} %taps_ref.1) | copy-start | bytes 496
  111.6 1.2 copy-start.1

commit v5 on v4

--- a/solution.py
+++ b/solution.py
@@ -27,17 +27,11 @@
 MESH = pl.DeviceIdType.MESH
 HALFWAY = ((2, 2), (2, 0), (0, 2), (2, 1), (1, 2), (2, 3), (3, 2))
 RELAYED = tuple((dx, 1, dy) for dx, dy in HALFWAY)
-EARLY = tuple(
+DIRECT = tuple((dx, 0, dy) for dx, dy in HALFWAY) + tuple(
     (dx, dc, dy)
-    for dx, dy in ((2, 2), (2, 0), (0, 2), (2, 1), (1, 2), (1, 1), (1, 0), (0, 1), (0, 0))
+    for dx, dy in ((1, 3), (3, 1), (1, 1), (3, 3), (1, 0), (3, 0), (0, 1), (0, 3), (0, 0))
     for dc in range(NC)
-    if (dx, dc, dy) != (0, 0, 0) and (dx, dc, dy) not in RELAYED
-)
-LATE = tuple(
-    (dx, dc, dy)
-    for dx, dy in ((2, 3), (3, 2), (3, 3), (1, 3), (3, 1), (3, 0), (0, 3))
-    for dc in range(NC)
-    if (dx, dc, dy) not in RELAYED
+    if (dx, dc, dy) != (0, 0, 0)
 )
 F32 = jnp.float32
 BF16 = jnp.bfloat16
@@ -181,7 +175,7 @@
     def at(place):
         return device(place[0], z, place[1], place[2])
 
-    everyone = RELAYED + EARLY + LATE
+    everyone = RELAYED + DIRECT
     barrier = pltpu.get_barrier_semaphore()
     for offset in everyone:
         pl.semaphore_signal(barrier, inc=1, device_id=at(moved(*offset)), device_id_type=MESH)
@@ -236,7 +230,7 @@
         copy.start()
         copies.append(copy)
 
-    for offset in EARLY:
+    for offset in DIRECT:
         send(offset)
     take.wait()
     put = pltpu.make_async_copy(own, in_ref.at[me], own_sem)
@@ -255,8 +249,6 @@
         )
         copy.start()
         copies.append(copy)
-    for offset in LATE:
-        send(offset)
     keep.wait()
     for copy in infos:
         copy.wait()
@@ -357,7 +349,7 @@
         in_specs=[smem, smem, pl.BlockSpec((per_step, SLOTS, STRIP, B), lambda i: (i, 0, 0, 0))],
         out_specs=pl.BlockSpec(shape, lambda i: (0, 0, 0)),
         scratch_shapes=[pltpu.VMEM(shape, F32)],
-        compiler_params=pltpu.CompilerParams(vmem_limit_bytes=60 * 1024 * 1024),
+        compiler_params=pltpu.CompilerParams(vmem_limit_bytes=16 * 1024 * 1024),
         name="gather_slots",
     )(cell, scale, arrived)
 

time: 157 us -> 150 us (0.955)
  Pallas kernels: 135 us -> 129 us
    pallas_call x1, Pallas kernels: 40.7 us -> 36.6 us  [detect(): pl.pallas_call(detect_kernel, out_shape=jax.ShapeDtypeStruct((B, CC * B),...]
    pallas_call x1, Pallas kernels: 9.24 us -> 7.17 us  [gather_slots(): pl.pallas_call(gather_kernel, grid=(PLANE // per_step,), out_shape=jax.Sh...]
where the time goes in v5:
time: 150 us; the launch traced here: 149 us
  Pallas kernels  129 us (86%)
  local copies, waits for them, and re-layouts  11.1 us (7%)
  other arithmetic  7.45 us (5%)
    pallas_call x1, Pallas kernels, plane_exchange(): pl.pallas_call(plane_kernel, out_shape=(jax.ShapeDtypeStruct((PLANE, SLOT...  72.7 us
    pallas_call x1, Pallas kernels, detect(): pl.pallas_call(detect_kernel, out_shape=jax.ShapeDtypeStruct((B, CC * B),...  36.6 us
    pallas_call x1, Pallas kernels, match(): pl.pallas_call(match_kernel, out_shape=jax.ShapeDtypeStruct((PLANE * SLOT...  12.6 us
    unnamed x16, local copies, waits for them, and re-layouts  7.68 us
    pallas_call x1, Pallas kernels, gather_slots(): pl.pallas_call(gather_kernel, grid=(PLANE // per_step,), out_shape=jax.Sh...  7.17 us

profile of v5, /device:TPU:16, one launch (start us, length us, event | category | flops | bytes accessed | tf_op | source)
XLA Modules:
  0.0 148.6 jit_solution(13198374582395124824)
XLA Ops:
  0.0 0.7 bitcast_convert_fusion
  0.7 0.9 convert_reduce_fusion
  1.6 0.7 fusion.19
  2.2 0.7 convert_bitcast_fusion.1
  2.9 0.7 convert_bitcast_fusion.2
  3.7 0.8 copy.21.coef_ref
  4.5 1.5 %copy-done.2 = bf16[168,5376]{1,0:T(8,128)(2,1)S(1)} copy-done((bf16[168,5376]{1,0:T(8,128)(2,1)S(1)}, bf16[168,5376]{1,0:T(8,128)(2,1)}, u32[]{:S(2)}) %copy-start.2) | copy-done | bytes 1806360
  5.9 0.7 copy-done.3
  6.6 0.7 copy-done.4
  7.3 12.6 %match.1 = bf16[512,32,128]{2,1,0:T(8,128)(2,1)S(1)} custom-call(s32[32]{0:T(128)S(1)} %get-tuple-element.9.slot_ref, f32[32,3]{1,0:T(8,128)S(1)} %copy.21.coef_ref, f32[3,41]{1,0:T(4,128)S(1)} %copy-done.3, f32[3,41]{1,0:T(4,128)S(1)} %copy-done.4, bf16[168,5376]{1,0:T(8,128)(2,1)S(1)} %copy-done.2), custom_call_target="tpu_custom_call" | custom-call | tf_op jit(solution)/shard_map/match/pallas_call | solution.py:128
  19.9 72.7 %plane_exchange.1 = (bf16[32,16,32,128]{3,2,1,0:T(8,128)(2,1)S(1)}, f32[8,32,1,128]{3,2,1,0:T(1,128)S(1)}) custom-call(bf16[32,16,32,128]{3,2,1,0:T(8,128)(2,1)S(1)} %bitcast.33, f32[1,1,128]{2,1,0:T(1,128)S(1)} %reshape.139.info_ref), custom_call_target="tpu_custom_call" | custom-call | tf_op jit(solution)/shard_map/plane_exchange/pallas_call | solution.py:280
  92.7 1.9 %copy-done = bf16[32,16,32,128]{3,2,1,0:T(8,128)(2,1)} copy-done((bf16[32,16,32,128]{3,2,1,0:T(8,128)(2,1)}, bf16[32,16,32,128]{3,2,1,0:T(8,128)(2,1)S(1)}, u32[]{:S(2)}) %copy-start) | copy-done | bytes 4194328
  94.6 0.5 broadcast.160
  95.1 1.0 reduce.15
  96.1 0.3 reshape.141
  96.5 0.1 broadcast_compare_fusion
  96.6 1.2 fusion.4
  97.9 0.1 copy.24
  98.0 0.1 sub.19.cell_ref
  98.2 0.8 fusion.7
  99.1 0.4 slice_reduce_fusion
  99.5 0.1 reshape_squeeze.3
  99.6 0.1 convert_element_type.72
  99.9 0.7 fusion.3
  100.8 0.5 select_reduce_fusion
  101.3 0.2 fusion.5
  101.4 0.3 copy.25
  101.7 0.1 reshape.143.scale_ref
  101.9 2.2 %copy-done.1 = bf16[32,16,32,128]{3,2,1,0:T(8,128)(2,1)S(1)} copy-done((bf16[32,16,32,128]{3,2,1,0:T(8,128)(2,1)S(1)}, bf16[32,16,32,128]{3,2,1,0:T(8,128)(2,1)}, u32[]{:S(2)}) %copy-start.1) | copy-done | bytes 4194328
  104.0 7.2 %gather_slots.1 = bf16[32,32,512]{2,1,0:T(8,128)(2,1)S(1)} custom-call(s32[512]{0:T(512)S(1)} %sub.19.cell_ref, f32[512]{0:T(512)S(1)} %reshape.143.scale_ref, bf16[32,16,32,128]{3,2,1,0:T(8,128)(2,1)S(1)} %copy-done.1), custom_call_target="tpu_custom_call" | custom-call | tf_op jit(solution)/shard_map/gather_slots/pallas_call | solution.py:345
  111.2 36.6 %detect.1 = f32[128,512]{1,0:T(8,128)S(1)} custom-call(f32[41]{0:T(128)S(1)} %copy-done.5, bf16[8,4,32,512]{3,2,1,0:T(8,128)(2,1)S(1)} %bitcast.34), custom_call_target="tpu_custom_call" | custom-call | tf_op jit(solution)/shard_map/detect/pallas_call | solution.py:543
  147.9 0.7 copy.30
  (27 shorter events, 0.7 us)
Async XLA Ops:
  4.4 1.5 %copy-start.2 = (bf16[168,5376]{1,0:T(8,128)(2,1)S(1)}, bf16[168,5376]{1,0:T(8,128)(2,1)}, u32[]{:S(2)}) copy-start(bf16[168,5376]{1,0:T(8,128)(2,1)} %raw_ref.1) | copy-start | bytes 5419012
  5.9 0.7 copy-start.3
  6.6 0.7 copy-start.4
  19.9 79.8 %copy-start.6 = (f32[6]{0:T(128)S(1)}, f32[6]{0:T(128)}, u32[]{:S(2)}) copy-start(f32[6]{0:T(128)} %param.18) | copy-start | bytes 76
  92.7 1.9 %copy-start = (bf16[32,16,32,128]{3,2,1,0:T(8,128)(2,1)}, bf16[32,16,32,128]{3,2,1,0:T(8,128)(2,1)S(1)}, u32[]{:S(2)}) copy-start(bf16[32,16,32,128]{3,2,1,0:T(8,128)(2,1)S(1)} %get-tuple-element.12.in_ref) | copy-start | bytes 12582916
  99.9 11.3 %copy-start.5 = (f32[41]{0:T(128)S(1)}, f32[41]{0:T(128)}, u32[]{:S(2)}) copy-start(f32[41]{0:T(128)} %taps_ref.1) | copy-start | bytes 496
  101.9 2.2 %copy-start.1 = (bf16[32,16,32,128]{3,2,1,0:T(8,128)(2,1)S(1)}, bf16[32,16,32,128]{3,2,1,0:T(8,128)(2,1)}, u32[]{:S(2)}) copy-start(bf16[32,16,32,128]{3,2,1,0:T(8,128)(2,1)} %copy-done) | copy-start | bytes 12582916

commit v6 on v5

--- a/solution.py
+++ b/solution.py
@@ -156,6 +156,7 @@
     recv_sem,
     pass_send,
     pass_recv,
+    relay_send,
     info_send,
     info_recv,
     z_send,
@@ -204,14 +205,21 @@
         copy.start()
         infos.append(copy)
     firsts = []
+    edge_x = NX - 1 - lax.rem(x, 2) * (NX - 1)
+    edge_y = NY - 1 - lax.rem(y, 2) * (NY - 1)
     for k, (dx, dc, dy) in enumerate(RELAYED):
-        back_x, back_y = (NX - 1) * (dx == 2), (NY - 1) * (dy == 2)
+        over_x, over_y = dx == 2, dy == 2
+        hold = k * 4
+        if over_x:
+            hold = hold + lax.div(x, 2) * 2
+        if over_y:
+            hold = hold + lax.div(y, 2)
         copy = pltpu.make_async_remote_copy(
             src_ref=out_ref.at[index(moved(dx, dc, dy))],
-            dst_ref=passing.at[k],
+            dst_ref=passing.at[hold],
             send_sem=pass_send.at[k],
-            recv_sem=pass_recv.at[k],
-            device_id=at(moved(back_x, 0, back_y)),
+            recv_sem=pass_recv.at[hold],
+            device_id=at((edge_x if over_x else x, core, edge_y if over_y else y)),
             device_id_type=MESH,
         )
         copy.start()
@@ -235,20 +243,50 @@
     take.wait()
     put = pltpu.make_async_copy(own, in_ref.at[me], own_sem)
     put.start()
-    for k, offset in enumerate(RELAYED):
-        dx, dc, dy = offset
-        ahead_x, ahead_y = dx == 2, dy == 2
-        firsts[k].wait_recv()
-        copy = pltpu.make_async_remote_copy(
-            src_ref=passing.at[k],
-            dst_ref=in_ref.at[index(moved(int(ahead_x), 0, int(ahead_y)))],
-            send_sem=send_sem.at[offset_id(offset)],
-            recv_sem=recv_sem.at[offset_id(offset)],
-            device_id=at(moved((dx + ahead_x) % NX, dc, (dy + ahead_y) % NY)),
-            device_id_type=MESH,
-        )
-        copy.start()
-        copies.append(copy)
+    def relay(k, jx, jy):
+        dx, dc, dy = RELAYED[k]
+        hold = k * 4 + jx * 2 + jy
+        from_x = jx * 2 + 1 - lax.div(x, NX - 1) if dx == 2 else x
+        from_y = jy * 2 + 1 - lax.div(y, NY - 1) if dy == 2 else y
+        dest = (lax.rem(from_x + dx, NX), lax.rem(core + dc, NC), lax.rem(from_y + dy, NY))
+        return pltpu.make_async_remote_copy(
+            src_ref=passing.at[hold],
+            dst_ref=in_ref.at[index((from_x, core, from_y))],
+            send_sem=relay_send.at[hold],
+            recv_sem=recv_sem.at[offset_id(RELAYED[k])],
+            device_id=at(dest),
+            device_id_type=MESH,
+        )
+
+    def arrival(k, jx, jy):
+        hold = k * 4 + jx * 2 + jy
+        return pltpu.make_async_remote_copy(
+            src_ref=out_ref.at[0],
+            dst_ref=passing.at[hold],
+            send_sem=pass_send.at[k],
+            recv_sem=pass_recv.at[hold],
+            device_id=at(moved(1, 0, 0)),
+            device_id_type=MESH,
+        )
+
+    def relays(act):
+        for k, (dx, dc, dy) in enumerate(RELAYED):
+            over_x, over_y = dx == 2, dy == 2
+            here_x = (x == 0) | (x == NX - 1)
+            here_y = (y == 0) | (y == NY - 1)
+            here = here_x & here_y if over_x and over_y else here_x if over_x else here_y
+
+            @pl.when(here)
+            def _():
+                for jx in range(2 if over_x else 1):
+                    for jy in range(2 if over_y else 1):
+                        act(k, jx, jy)
+
+    def forward(k, jx, jy):
+        arrival(k, jx, jy).wait_recv()
+        relay(k, jx, jy).start()
+
+    relays(forward)
     keep.wait()
     for copy in infos:
         copy.wait()
@@ -269,6 +307,16 @@
         copy.wait()
     for copy in firsts:
         copy.wait_send()
+    relays(lambda k, jx, jy: relay(k, jx, jy).wait_send())
+    for offset in RELAYED:
+        pltpu.make_async_remote_copy(
+            src_ref=out_ref.at[0],
+            dst_ref=in_ref.at[index(moved(NX - offset[0], NC - offset[1], NY - offset[2]))],
+            send_sem=send_sem.at[0],
+            recv_sem=recv_sem.at[offset_id(offset)],
+            device_id=at(moved(1, 0, 0)),
+            device_id_type=MESH,
+        ).wait_recv()
     for copy in copies:
         copy.wait()
 
@@ -287,11 +335,12 @@
         out_specs=(pl.BlockSpec(memory_space=pltpu.HBM), vmem),
         scratch_shapes=[
             pltpu.VMEM((SLOTS, STRIP, B), BF16),
-            pltpu.VMEM((len(RELAYED), SLOTS, STRIP, B), BF16),
+            pltpu.VMEM((4 * len(RELAYED), SLOTS, STRIP, B), BF16),
             dma((PLANE,)),
             dma((PLANE,)),
             dma((len(RELAYED),)),
-            dma((len(RELAYED),)),
+            dma((4 * len(RELAYED),)),
+            dma((4 * len(RELAYED),)),
             dma((PLANE,)),
             dma((PLANE,)),
             dma((NZ,)),
@@ -300,7 +349,7 @@
             dma,
         ],
         compiler_params=pltpu.CompilerParams(
-            collective_id=0, has_side_effects=True, vmem_limit_bytes=4 * 1024 * 1024
+            collective_id=0, has_side_effects=True, vmem_limit_bytes=8 * 1024 * 1024
         ),
         name="plane_exchange",
     )(outgoing, info)

time: 150 us -> 155 us (1.033)
  Pallas kernels: 129 us -> 135 us
    pallas_call x1, Pallas kernels: 72.7 us -> 76.2 us  [plane_exchange(): pl.pallas_call(plane_kernel, out_shape=(jax.ShapeDtypeStruct((PLANE, SLOT...]
    pallas_call x1, Pallas kernels: 36.6 us -> 39.6 us  [detect(): pl.pallas_call(detect_kernel, out_shape=jax.ShapeDtypeStruct((B, CC * B),...]
where the time goes in v6:
time: 155 us; the launch traced here: 154 us
  Pallas kernels  135 us (87%)
  local copies, waits for them, and re-layouts  11.1 us (7%)
  other arithmetic  7.45 us (5%)
    pallas_call x1, Pallas kernels, plane_exchange(): pl.pallas_call(plane_kernel, out_shape=(jax.ShapeDtypeStruct((PLANE, SLOT...  76.2 us
    pallas_call x1, Pallas kernels, detect(): pl.pallas_call(detect_kernel, out_shape=jax.ShapeDtypeStruct((B, CC * B),...  39.6 us
    pallas_call x1, Pallas kernels, match(): pl.pallas_call(match_kernel, out_shape=jax.ShapeDtypeStruct((PLANE * SLOT...  12.6 us
    unnamed x16, local copies, waits for them, and re-layouts  7.68 us
    pallas_call x1, Pallas kernels, gather_slots(): pl.pallas_call(gather_kernel, grid=(PLANE // per_step,), out_shape=jax.Sh...  6.42 us

profile of v6, /device:TPU:16, one launch (start us, length us, event | category | flops | bytes accessed | tf_op | source)
XLA Modules:
  0.0 154.3 jit_solution(14968563670542758978)
XLA Ops:
  0.0 0.7 bitcast_convert_fusion
  0.7 0.9 convert_reduce_fusion
  1.6 0.7 fusion.19
  2.2 0.7 convert_bitcast_fusion.1
  2.9 0.7 convert_bitcast_fusion.2
  3.7 0.8 copy.21.coef_ref
  4.5 1.5 copy-done.2
  5.9 0.7 copy-done.3
  6.6 0.7 copy-done.4
  7.3 12.6 %match.1 = bf16[512,32,128]{2,1,0:T(8,128)(2,1)S(1)} custom-call(s32[32]{0:T(128)S(1)} %get-tuple-element.9.slot_ref, f32[32,3]{1,0:T(8,128)S(1)} %copy.21.coef_ref, f32[3,41]{1,0:T(4,128)S(1)} %copy-done.3, f32[3,41]{1,0:T(4,128)S(1)} %copy-done.4, bf16[168,5376]{1,0:T(8,128)(2,1)S(1)} %copy-done.2), custom_call_target="tpu_custom_call" | custom-call | tf_op jit(solution)/shard_map/match/pallas_call | solution.py:128
  19.9 76.2 %plane_exchange.1 = (bf16[32,16,32,128]{3,2,1,0:T(8,128)(2,1)S(1)}, f32[8,32,1,128]{3,2,1,0:T(1,128)S(1)}) custom-call(bf16[32,16,32,128]{3,2,1,0:T(8,128)(2,1)S(1)} %bitcast.33, f32[1,1,128]{2,1,0:T(1,128)S(1)} %reshape.139.info_ref), custom_call_target="tpu_custom_call" | custom-call | tf_op jit(solution)/shard_map/plane_exchange/pallas_call | solution.py:328
  96.2 1.9 %copy-done = bf16[32,16,32,128]{3,2,1,0:T(8,128)(2,1)} copy-done((bf16[32,16,32,128]{3,2,1,0:T(8,128)(2,1)}, bf16[32,16,32,128]{3,2,1,0:T(8,128)(2,1)S(1)}, u32[]{:S(2)}) %copy-start) | copy-done | bytes 4194328
  98.1 0.5 broadcast.160
  98.6 1.0 reduce.15
  99.6 0.3 reshape.141
  100.0 0.1 broadcast_compare_fusion
  100.1 1.2 fusion.4
  101.4 0.1 copy.24
  101.5 0.1 sub.19.cell_ref
  101.6 0.8 fusion.7
  102.6 0.4 slice_reduce_fusion
  103.0 0.1 reshape_squeeze.3
  103.1 0.1 convert_element_type.72
  103.4 0.7 fusion.3
  104.3 0.5 select_reduce_fusion
  104.7 0.2 fusion.5
  104.9 0.3 copy.25
  105.2 0.1 reshape.143.scale_ref
  105.3 2.2 %copy-done.1 = bf16[32,16,32,128]{3,2,1,0:T(8,128)(2,1)S(1)} copy-done((bf16[32,16,32,128]{3,2,1,0:T(8,128)(2,1)S(1)}, bf16[32,16,32,128]{3,2,1,0:T(8,128)(2,1)}, u32[]{:S(2)}) %copy-start.1) | copy-done | bytes 4194328
  107.5 6.4 %gather_slots.1 = bf16[32,32,512]{2,1,0:T(8,128)(2,1)S(1)} custom-call(s32[512]{0:T(512)S(1)} %sub.19.cell_ref, f32[512]{0:T(512)S(1)} %reshape.143.scale_ref, bf16[32,16,32,128]{3,2,1,0:T(8,128)(2,1)S(1)} %copy-done.1), custom_call_target="tpu_custom_call" | custom-call | tf_op jit(solution)/shard_map/gather_slots/pallas_call | solution.py:394
  114.0 39.6 %detect.1 = f32[128,512]{1,0:T(8,128)S(1)} custom-call(f32[41]{0:T(128)S(1)} %copy-done.5, bf16[8,4,32,512]{3,2,1,0:T(8,128)(2,1)S(1)} %bitcast.34), custom_call_target="tpu_custom_call" | custom-call | tf_op jit(solution)/shard_map/detect/pallas_call | solution.py:592
  153.6 0.7 copy.30
  (27 shorter events, 0.7 us)
Async XLA Ops:
  4.4 1.5 copy-start.2
  5.9 0.7 copy-start.3
  6.6 0.7 copy-start.4
  19.9 83.3 %copy-start.6 = (f32[6]{0:T(128)S(1)}, f32[6]{0:T(128)}, u32[]{:S(2)}) copy-start(f32[6]{0:T(128)} %param.18) | copy-start | bytes 76
  96.2 1.9 %copy-start = (bf16[32,16,32,128]{3,2,1,0:T(8,128)(2,1)}, bf16[32,16,32,128]{3,2,1,0:T(8,128)(2,1)S(1)}, u32[]{:S(2)}) copy-start(bf16[32,16,32,128]{3,2,1,0:T(8,128)(2,1)S(1)} %get-tuple-element.12.in_ref) | copy-start | bytes 12582916
  103.4 10.6 %copy-start.5 = (f32[41]{0:T(128)S(1)}, f32[41]{0:T(128)}, u32[]{:S(2)}) copy-start(f32[41]{0:T(128)} %taps_ref.1) | copy-start | bytes 496
  105.3 2.2 %copy-start.1 = (bf16[32,16,32,128]{3,2,1,0:T(8,128)(2,1)S(1)}, bf16[32,16,32,128]{3,2,1,0:T(8,128)(2,1)}, u32[]{:S(2)}) copy-start(bf16[32,16,32,128]{3,2,1,0:T(8,128)(2,1)} %copy-done) | copy-start | bytes 12582916

commit v7 on v5

--- a/solution.py
+++ b/solution.py
@@ -592,7 +592,9 @@
     patch = patch_of_block[:, 0]
     rank = ranks(patch)
     target = band_of_block * CELLS + cell_of_block
-    own_details = jnp.stack([v.astype(F32) for v in (patch, target, rank, block_weight)])
+    field = jnp.arange(4, dtype=jnp.int32)[:, None]
+    names = jnp.where(field == 0, patch, jnp.where(field == 1, target, rank))
+    own_details = jnp.where(field == 3, block_weight.astype(F32), names.astype(F32))
     patch_core = patch % NC
     patch_z = patch // NC % NZ
     patch_x = patch // (NC * NZ)

time: 150 us -> 151 us (level)
    pallas_call x1, Pallas kernels: 36.6 us -> 38.7 us  [detect(): pl.pallas_call(detect_kernel, out_shape=jax.ShapeDtypeStruct((B, CC * B),...]
where the time goes in v7:
time: 151 us; the launch traced here: 150 us
  Pallas kernels  130 us (86%)
  local copies, waits for them, and re-layouts  11.1 us (7%)
  other arithmetic  7.52 us (5%)
    pallas_call x1, Pallas kernels, plane_exchange(): pl.pallas_call(plane_kernel, out_shape=(jax.ShapeDtypeStruct((PLANE, SLOT...  72.8 us
    pallas_call x1, Pallas kernels, detect(): pl.pallas_call(detect_kernel, out_shape=jax.ShapeDtypeStruct((B, CC * B),...  38.7 us
    pallas_call x1, Pallas kernels, match(): pl.pallas_call(match_kernel, out_shape=jax.ShapeDtypeStruct((PLANE * SLOT...  12.6 us
    unnamed x16, local copies, waits for them, and re-layouts  7.68 us
    pallas_call x1, Pallas kernels, gather_slots(): pl.pallas_call(gather_kernel, grid=(PLANE // per_step,), out_shape=jax.Sh...  6.39 us

profile of v7, /device:TPU:16, one launch (start us, length us, event | category | flops | bytes accessed | tf_op | source)
XLA Modules:
  0.0 150.0 jit_solution(4448196913270043862)
XLA Ops:
  0.0 0.9 convert_reduce_fusion
  0.9 0.7 multiply_add_fusion.2
  1.6 0.7 convert_element_type.47
  2.3 0.7 convert_select_fusion
  3.1 0.7 fusion.19.slot_ref
  3.8 0.8 copy.21.coef_ref
  4.5 1.5 copy-done.2
  6.0 0.7 copy-done.3
  6.7 0.7 copy-done.4
  7.4 12.6 %match.1 = bf16[512,32,128]{2,1,0:T(8,128)(2,1)S(1)} custom-call(s32[32]{0:T(128)S(1)} %fusion.19.slot_ref, f32[32,3]{1,0:T(8,128)S(1)} %copy.21.coef_ref, f32[3,41]{1,0:T(4,128)S(1)} %copy-done.3, f32[3,41]{1,0:T(4,128)S(1)} %copy-done.4, bf16[168,5376]{1,0:T(8,128)(2,1)S(1)} %copy-done.2), custom_call_target="tpu_custom_call" | custom-call | tf_op jit(solution)/shard_map/match/pallas_call | solution.py:128
  20.0 72.8 %plane_exchange.1 = (bf16[32,16,32,128]{3,2,1,0:T(8,128)(2,1)S(1)}, f32[8,32,1,128]{3,2,1,0:T(1,128)S(1)}) custom-call(bf16[32,16,32,128]{3,2,1,0:T(8,128)(2,1)S(1)} %bitcast.24, f32[1,1,128]{2,1,0:T(1,128)S(1)} %select_n.90.info_ref), custom_call_target="tpu_custom_call" | custom-call | tf_op jit(solution)/shard_map/plane_exchange/pallas_call | solution.py:280
  92.8 1.9 %copy-done = bf16[32,16,32,128]{3,2,1,0:T(8,128)(2,1)} copy-done((bf16[32,16,32,128]{3,2,1,0:T(8,128)(2,1)}, bf16[32,16,32,128]{3,2,1,0:T(8,128)(2,1)S(1)}, u32[]{:S(2)}) %copy-start) | copy-done | bytes 4194328
  94.7 0.5 broadcast.204
  95.2 1.0 reduce.15
  96.2 0.3 reshape.213
  96.6 0.1 broadcast_compare_fusion
  96.7 1.2 fusion.4
  98.0 0.1 copy.24
  98.2 0.1 sub.19.cell_ref
  98.3 0.8 fusion.7
  99.2 0.4 slice_reduce_fusion
  99.7 0.1 reshape_squeeze.3
  99.8 0.1 convert_element_type.53
  100.0 0.7 fusion.3
  100.9 0.5 select_reduce_fusion
  101.4 0.2 fusion.5
  101.6 0.3 copy.25
  101.8 0.1 reshape.215.scale_ref
  102.0 2.2 %copy-done.1 = bf16[32,16,32,128]{3,2,1,0:T(8,128)(2,1)S(1)} copy-done((bf16[32,16,32,128]{3,2,1,0:T(8,128)(2,1)S(1)}, bf16[32,16,32,128]{3,2,1,0:T(8,128)(2,1)}, u32[]{:S(2)}) %copy-start.1) | copy-done | bytes 4194328
  104.2 6.4 %gather_slots.1 = bf16[32,32,512]{2,1,0:T(8,128)(2,1)S(1)} custom-call(s32[512]{0:T(512)S(1)} %sub.19.cell_ref, f32[512]{0:T(512)S(1)} %reshape.215.scale_ref, bf16[32,16,32,128]{3,2,1,0:T(8,128)(2,1)S(1)} %copy-done.1), custom_call_target="tpu_custom_call" | custom-call | tf_op jit(solution)/shard_map/gather_slots/pallas_call | solution.py:345
  110.6 38.7 %detect.1 = f32[128,512]{1,0:T(8,128)S(1)} custom-call(f32[41]{0:T(128)S(1)} %copy-done.5, bf16[8,4,32,512]{3,2,1,0:T(8,128)(2,1)S(1)} %bitcast.25), custom_call_target="tpu_custom_call" | custom-call | tf_op jit(solution)/shard_map/detect/pallas_call | solution.py:543
  149.3 0.7 copy.30
  (28 shorter events, 0.7 us)
Async XLA Ops:
  4.5 1.5 copy-start.2
  6.0 0.7 copy-start.3
  6.7 0.7 copy-start.4
  20.0 79.9 %copy-start.6 = (f32[6]{0:T(128)S(1)}, f32[6]{0:T(128)}, u32[]{:S(2)}) copy-start(f32[6]{0:T(128)} %param.18) | copy-start | bytes 76
  92.8 1.9 %copy-start = (bf16[32,16,32,128]{3,2,1,0:T(8,128)(2,1)}, bf16[32,16,32,128]{3,2,1,0:T(8,128)(2,1)S(1)}, u32[]{:S(2)}) copy-start(bf16[32,16,32,128]{3,2,1,0:T(8,128)(2,1)S(1)} %get-tuple-element.12.in_ref) | copy-start | bytes 12582916
  100.0 10.5 %copy-start.5 = (f32[41]{0:T(128)S(1)}, f32[41]{0:T(128)}, u32[]{:S(2)}) copy-start(f32[41]{0:T(128)} %taps_ref.1) | copy-start | bytes 496
  102.0 2.2 %copy-start.1 = (bf16[32,16,32,128]{3,2,1,0:T(8,128)(2,1)S(1)}, bf16[32,16,32,128]{3,2,1,0:T(8,128)(2,1)}, u32[]{:S(2)}) copy-start(bf16[32,16,32,128]{3,2,1,0:T(8,128)(2,1)} %copy-done) | copy-start | bytes 12582916
